TPU v7x, 128 devices: a whole 4x4x4 slice. The times are simulated.
128 devices in a mesh: rows: 16 (over z, y_hi, core), grp: 8 (over y_lo, x).
Axes of the slice: x: 4, y: 4 (y_hi: 2, y_lo: 2; y = y_hi * 2 + y_lo), z: 4, core: 2. Of those that a mesh axis runs over, the one named last changes fastest.
Arguments:
- sorted_rows: bfloat16 [32768, 2048], P(('rows', 'grp')), may hold values from -6 to 6
- combine: bfloat16 [32768], P(('rows', 'grp')), may hold values from 0.099609375 to 1
- cotangent: bfloat16 [32768, 2048], P(('rows', 'grp')), may hold values from -6 to 6
- starts: int32 [128], P(('rows', 'grp')), may hold values from 0 to 32767, as said below
- w_gate: bfloat16 [128, 2048, 768], P(('rows', 'grp')), may hold values from -0.125 to 0.125
- w_up: bfloat16 [128, 2048, 768], P(('rows', 'grp')), may hold values from -0.125 to 0.125
- w_down: bfloat16 [128, 768, 2048], P(('rows', 'grp')), may hold values from -0.21875 to 0.21875
Outputs:
- mixed: bfloat16 [32768, 2048], P(('rows', 'grp'))
- combine_grad: bfloat16 [32768], P(('rows', 'grp'))
- input_grad: bfloat16 [32768, 2048], P(('rows', 'grp'))
- grad_gate: bfloat16 [128, 2048, 768], P(('rows', 'grp'))
- grad_up: bfloat16 [128, 2048, 768], P(('rows', 'grp'))
- grad_down: bfloat16 [128, 768, 2048], P(('rows', 'grp'))
Inputs may be any that keep to these rules, and one draw needn't show every extreme that they name: starts[e] is the first sorted row of expert e; starts[0] = 0, starts[127] = 32767, and 256 * e < starts[e] < 256 * (e + 1) for e >= 1, so the rows of expert e lie in shards e and e + 1 of 256 rows, and every shard after the first begins with rows of the previous expert.
All inputs are finite; a program needn't handle non-finite values.
Results may differ from a plain program's by a relative error of at most 0.0058.
Values may be sent and summed in bfloat16 or wider, within the bound.
A program may use at most 128 MiB of HBM per device.

v0:
```python
import jax
import jax.numpy as jnp
from jax import lax
from jax.sharding import PartitionSpec as P


def from_behind(block, axis, distance):
    devices = range(lax.axis_size(axis))
    route = [(i - distance, i) for i in devices if i - distance in devices]
    return lax.ppermute(block, axis, route)


def contract_rows(left, right):
    return lax.dot_general(
        left, right, (((0,), (0,)), ((), ())), preferred_element_type=jnp.float32
    )


def contract_cols(left, right):
    return lax.dot_general(
        left, right, (((1,), (1,)), ((), ())), preferred_element_type=jnp.float32
    )


def run_expert(rows_in, combine_rows, cotan_rows, keep, gate_w, up_w, down_w):
    gate_pre = jnp.dot(rows_in, gate_w, preferred_element_type=jnp.float32)
    up_pre = jnp.dot(rows_in, up_w, preferred_element_type=jnp.float32)
    sig_gate = jax.nn.sigmoid(gate_pre)
    silu_gate = gate_pre * sig_gate
    hidden = (silu_gate * up_pre).astype(jnp.bfloat16)
    expert_out = jnp.dot(hidden, down_w, preferred_element_type=jnp.float32)
    scale_col = combine_rows.astype(jnp.float32)[:, None]
    mixed = (scale_col * expert_out).astype(jnp.bfloat16)
    comb_grad = jnp.sum(expert_out * cotan_rows.astype(jnp.float32), axis=1).astype(jnp.bfloat16)
    out_grad = (scale_col * cotan_rows.astype(jnp.float32)).astype(jnp.bfloat16)
    out_grad = jnp.where(keep[:, None], out_grad, jnp.zeros_like(out_grad))
    hidden_grad = contract_cols(out_grad, down_w)
    gate_grad = (hidden_grad * up_pre * sig_gate * (1.0 + gate_pre * (1.0 - sig_gate))).astype(
        jnp.bfloat16
    )
    up_grad = (hidden_grad * silu_gate).astype(jnp.bfloat16)
    in_grad = (contract_cols(gate_grad, gate_w) + contract_cols(up_grad, up_w)).astype(jnp.bfloat16)
    gate_wgrad = contract_rows(rows_in, gate_grad)
    up_wgrad = contract_rows(rows_in, up_grad)
    down_wgrad = contract_rows(hidden, out_grad)
    return (mixed, comb_grad, in_grad, gate_wgrad, up_wgrad, down_wgrad)


def on_device(sorted_rows, combine, cotangent, starts, w_gate, w_up, w_down):
    count_rows = sorted_rows.shape[0]
    lead_count = jnp.remainder(starts[0], count_rows)
    lead_mask = jnp.arange(count_rows, dtype=jnp.int32) < lead_count
    own_mask = jnp.logical_not(lead_mask)
    previous = from_behind((w_gate, w_up, w_down), ("rows", "grp"), 1)
    own_part = run_expert(sorted_rows, combine, cotangent, own_mask, w_gate[0], w_up[0], w_down[0])
    lead_part = run_expert(
        sorted_rows, combine, cotangent, lead_mask, previous[0][0], previous[1][0], previous[2][0]
    )
    returned = from_behind(
        (lead_part[3][None], lead_part[4][None], lead_part[5][None]), ("rows", "grp"), -1
    )
    grad_gate = (own_part[3][None] + returned[0]).astype(jnp.bfloat16)
    grad_up = (own_part[4][None] + returned[1]).astype(jnp.bfloat16)
    grad_down = (own_part[5][None] + returned[2]).astype(jnp.bfloat16)
    mixed = jnp.where(lead_mask[:, None], lead_part[0], own_part[0])
    comb_grad = jnp.where(lead_mask, lead_part[1], own_part[1])
    in_grad = jnp.where(lead_mask[:, None], lead_part[2], own_part[2])
    return (mixed, comb_grad, in_grad, grad_gate, grad_up, grad_down)


def solution(mesh):
    in_specs = (
        P(("rows", "grp"), None),
        P(("rows", "grp")),
        P(("rows", "grp"), None),
        P(("rows", "grp")),
        P(("rows", "grp"), None, None),
        P(("rows", "grp"), None, None),
        P(("rows", "grp"), None, None),
    )
    out_specs = (
        P(("rows", "grp"), None),
        P(("rows", "grp")),
        P(("rows", "grp"), None),
        P(("rows", "grp"), None, None),
        P(("rows", "grp"), None, None),
        P(("rows", "grp"), None, None),
    )
    return jax.shard_map(
        on_device, mesh=mesh, in_specs=in_specs, out_specs=out_specs, check_vma=False
    )
```

profile of v0, /device:TPU:96, one launch (start us, length us, event | category | flops | bytes accessed | tf_op | source)
XLA Modules:
  0.0 628.6 jit_solution(8936563428309318619)
XLA Ops:
  0.6 0.0 copy-start
  0.6 0.0 copy-start.1
  0.7 3.5 collective-permute-start.1
  4.2 3.4 collective-permute-start.2
  7.6 3.1 collective-permute-start
  11.4 0.7 convert_element_type.59
  12.0 65.5 %collective-permute-done.1 = bf16[1,2048,768]{2,1,0:T(8,128)(2,1)} collective-permute-done((bf16[1,2048,768]{2,1,0:T(8,128)(2,1)}, bf16[1,2048,768]{2,1,0:T(8,128)(2,1)}, u32[]{:S(2)}, u32[]{:S(2)}) %collective-permute-start.1) | collective-permute-done | bytes 3145760 | tf_op jit(solution)/shard_map/ppermute | solution.py:10
  77.5 0.0 copy-done
  77.5 2.9 fusion.21
  80.4 64.5 %collective-permute-done.2 = bf16[1,768,2048]{2,1,0:T(8,128)(2,1)} collective-permute-done((bf16[1,768,2048]{2,1,0:T(8,128)(2,1)}, bf16[1,768,2048]{2,1,0:T(8,128)(2,1)}, u32[]{:S(2)}, u32[]{:S(2)}) %collective-permute-start.2) | collective-permute-done | bytes 3145760 | tf_op jit(solution)/shard_map/ppermute | solution.py:10
  145.0 0.0 copy-done.1
  145.0 2.9 fusion.15
  147.9 64.0 %collective-permute-done = bf16[1,2048,768]{2,1,0:T(8,128)(2,1)} collective-permute-done((bf16[1,2048,768]{2,1,0:T(8,128)(2,1)}, bf16[1,2048,768]{2,1,0:T(8,128)(2,1)}, u32[]{:S(2)}, u32[]{:S(2)}) %collective-permute-start) | collective-permute-done | bytes 3145760 | tf_op jit(solution)/shard_map/ppermute | solution.py:10
  211.9 3.1 multiply_convert_fusion.5
  215.0 1.0 convolution_bitcast_fusion.2
  216.1 1.9 collective-permute-start.3
  218.0 3.7 convolution_bitcast_fusion.1
  221.7 1.9 collective-permute-start.4
  223.6 0.0 copy-start.4
  223.6 3.7 convolution_bitcast_fusion
  227.3 0.0 copy-start.3
  227.3 2.5 collective-permute-start.5
  229.8 0.0 copy-done.4
  229.8 1.0 fusion.9
  230.8 0.0 copy-done.3
  230.8 0.0 copy-start.2
  230.8 1.0 fusion.3
  231.9 0.8 copy-done.2
  232.7 1.3 multiply_convert_fusion.3
  234.0 1.0 fusion.5
  235.0 1.0 fusion.7
  236.1 1.0 fusion.33
  237.1 4.0 fusion.45
  241.1 0.6 fusion.42
  241.7 0.5 convert_select_fusion
  242.2 2.9 fusion.19
  245.1 3.9 fusion.39
  249.0 107.3 %collective-permute-done.3 = f32[1,2048,768]{1,2,0:T(8,128)S(1)} collective-permute-done((f32[1,2048,768]{1,2,0:T(8,128)S(1)}, f32[1,2048,768]{1,2,0:T(8,128)S(1)}, u32[]{:S(2)}, u32[]{:S(2)}) %collective-permute-start.3) | collective-permute-done | bytes 6291488 | tf_op jit(solution)/shard_map/ppermute | solution.py:10
  356.4 2.7 fusion.1
  359.1 4.6 copy.13
  363.8 127.6 %collective-permute-done.4 = f32[1,2048,768]{1,2,0:T(8,128)} collective-permute-done((f32[1,2048,768]{1,2,0:T(8,128)}, f32[1,2048,768]{1,2,0:T(8,128)}, u32[]{:S(2)}, u32[]{:S(2)}) %collective-permute-start.4) | collective-permute-done | bytes 6291488 | tf_op jit(solution)/shard_map/ppermute | solution.py:10
  491.3 5.5 fusion
  496.8 4.6 copy.14
  501.4 121.6 %collective-permute-done.5 = f32[1,768,2048]{2,1,0:T(8,128)} collective-permute-done((f32[1,768,2048]{2,1,0:T(8,128)}, f32[1,768,2048]{2,1,0:T(8,128)}, u32[]{:S(2)}, u32[]{:S(2)}) %collective-permute-start.5) | collective-permute-done | bytes 6291488 | tf_op jit(solution)/shard_map/ppermute | solution.py:10
  623.0 5.6 fusion.2
  (2 shorter events, 0.0 us)
Async XLA Ops:
  0.6 76.9 %copy-start = (bf16[256,2048]{1,0:T(8,128)(2,1)S(1)}, bf16[256,2048]{1,0:T(8,128)(2,1)}, u32[]{:S(2)}) copy-start(bf16[256,2048]{1,0:T(8,128)(2,1)} %param.7) | copy-start | bytes 3145732
  0.6 144.3 %copy-start.1 = (bf16[256,2048]{1,0:T(8,128)(2,1)S(1)}, bf16[256,2048]{1,0:T(8,128)(2,1)}, u32[]{:S(2)}) copy-start(bf16[256,2048]{1,0:T(8,128)(2,1)} %param.9) | copy-start | bytes 3145732
  0.7 76.9 %collective-permute-start.1 = (bf16[1,2048,768]{2,1,0:T(8,128)(2,1)}, bf16[1,2048,768]{2,1,0:T(8,128)(2,1)}, u32[]{:S(2)}, u32[]{:S(2)}) collective-permute-start(bf16[1,2048,768]{2,1,0:T(8,128)(2,1)} %param.12), channel_id=1, source_target_pairs={{0,1},{1,2},{2,3},{3,4},{4,5},{5,6},{6,7},{7,8},{8,9},{9,10},{10,1... | collective-permute-start | bytes 9437192 | tf_op jit(solution)/shard_map/ppermute | solution.py:10
  4.2 140.8 %collective-permute-start.2 = (bf16[1,768,2048]{2,1,0:T(8,128)(2,1)}, bf16[1,768,2048]{2,1,0:T(8,128)(2,1)}, u32[]{:S(2)}, u32[]{:S(2)}) collective-permute-start(bf16[1,768,2048]{2,1,0:T(8,128)(2,1)} %param.13), channel_id=1, source_target_pairs={{0,1},{1,2},{2,3},{3,4},{4,5},{5,6},{6,7},{7,8},{8,9},{9,10},{10,1... | collective-permute-start | bytes 9437192 | tf_op jit(solution)/shard_map/ppermute | solution.py:10
  7.6 204.3 %collective-permute-start = (bf16[1,2048,768]{2,1,0:T(8,128)(2,1)}, bf16[1,2048,768]{2,1,0:T(8,128)(2,1)}, u32[]{:S(2)}, u32[]{:S(2)}) collective-permute-start(bf16[1,2048,768]{2,1,0:T(8,128)(2,1)} %param.11), channel_id=1, source_target_pairs={{0,1},{1,2},{2,3},{3,4},{4,5},{5,6},{6,7},{7,8},{8,9},{9,10},{10,1... | collective-permute-start | bytes 9437192 | tf_op jit(solution)/shard_map/ppermute | solution.py:10
  216.1 140.3 %collective-permute-start.3 = (f32[1,2048,768]{1,2,0:T(8,128)S(1)}, f32[1,2048,768]{1,2,0:T(8,128)S(1)}, u32[]{:S(2)}, u32[]{:S(2)}) collective-permute-start(f32[1,2048,768]{1,2,0:T(8,128)S(1)} %convolution_bitcast_fusion.2), channel_id=1, source_target_pairs={{1,0},{2,1},{3,2},{4,3},{5,4},{6,5},{7,6},{8,7},{9,8},{10,9},{11,1... | collective-permute-start | bytes 18874376 | tf_op jit(solution)/shard_map/ppermute | solution.py:10
  221.7 269.7 %collective-permute-start.4 = (f32[1,2048,768]{1,2,0:T(8,128)}, f32[1,2048,768]{1,2,0:T(8,128)}, u32[]{:S(2)}, u32[]{:S(2)}) collective-permute-start(f32[1,2048,768]{1,2,0:T(8,128)} %convolution_bitcast_fusion.1), channel_id=1, source_target_pairs={{1,0},{2,1},{3,2},{4,3},{5,4},{6,5},{7,6},{8,7},{9,8},{10,9},{11,1... | collective-permute-start | bytes 18874376 | tf_op jit(solution)/shard_map/ppermute | solution.py:10
  223.6 6.2 copy-start.4
  227.3 3.5 copy-start.3
  227.3 395.7 %collective-permute-start.5 = (f32[1,768,2048]{2,1,0:T(8,128)}, f32[1,768,2048]{2,1,0:T(8,128)}, u32[]{:S(2)}, u32[]{:S(2)}) collective-permute-start(f32[1,768,2048]{2,1,0:T(8,128)} %convolution_bitcast_fusion), channel_id=1, source_target_pairs={{1,0},{2,1},{3,2},{4,3},{5,4},{6,5},{7,6},{8,7},{9,8},{10,9},{11,1... | collective-permute-start | bytes 18874376 | tf_op jit(solution)/shard_map/ppermute | solution.py:10
  230.8 1.9 copy-start.2
where the time goes:
time: 631 us; the launch traced here: 629 us
  waiting for transfers between devices  551 us (87%)
  matrix products  48.2 us (8%)
  starting transfers between devices  16.4 us (3%)
  local copies, waits for them, and re-layouts  10.1 us (2%)
    ppermute x6, waiting for transfers between devices, from_behind(): return lax.ppermute(block, axis, route)  551 us
    dot_general x6, matrix products, contract_rows(): lax.dot_general(left, right, (((0,), (0,)), ((), ())), preferred_element_...  22.2 us
    ppermute x6, starting transfers between devices, from_behind(): return lax.ppermute(block, axis, route)  16.4 us
    dot_general x6, matrix products, contract_cols(): lax.dot_general(left, right, (((1,), (1,)), ((), ())), preferred_element_...  12.8 us
  transfers between devices with their start and end apart: 6, of which 6 were waited for; matrix products, arithmetic and copies ran while one was open for 8% of the time, Pallas kernels for 0%

commit v1 on v0

v1 whole, which is shorter than its diff:
```python
import jax
import jax.numpy as jnp
from jax import lax
from jax.sharding import PartitionSpec as P

AXES = ("rows", "grp")
X_CHUNKS = 2
C_CHUNKS = 4


def shift(block, distance):
    count = lax.axis_size(AXES)
    return lax.ppermute(block, AXES, [(i, (i + distance) % count) for i in range(count)])


def contract_rows(left, right):
    return lax.dot_general(
        left, right, (((0,), (0,)), ((), ())), preferred_element_type=jnp.float32
    )


def contract_cols(left, right):
    return lax.dot_general(
        left, right, (((1,), (1,)), ((), ())), preferred_element_type=jnp.float32
    )


def forward(rows_in, scale_col, gate_w, up_w, down_w):
    gate_pre = jnp.dot(rows_in, gate_w, preferred_element_type=jnp.float32)
    up_pre = jnp.dot(rows_in, up_w, preferred_element_type=jnp.float32)
    sig_gate = jax.nn.sigmoid(gate_pre)
    hidden = (gate_pre * sig_gate * up_pre).astype(jnp.bfloat16)
    expert_out = jnp.dot(hidden, down_w, preferred_element_type=jnp.float32)
    mixed = (scale_col * expert_out).astype(jnp.bfloat16)
    return gate_pre, up_pre, hidden, expert_out, mixed


def backward(cotan, scale_col, gate_pre, up_pre, expert_out, gate_w, up_w, down_w):
    cotan = cotan.astype(jnp.float32)
    comb_grad = jnp.sum(expert_out * cotan, axis=1)
    out_grad = (scale_col * cotan).astype(jnp.bfloat16)
    hidden_grad = contract_cols(out_grad, down_w)
    sig_gate = jax.nn.sigmoid(gate_pre)
    gate_grad = (hidden_grad * up_pre * sig_gate * (1.0 + gate_pre * (1.0 - sig_gate))).astype(
        jnp.bfloat16
    )
    up_grad = (hidden_grad * (gate_pre * sig_gate)).astype(jnp.bfloat16)
    in_grad = (contract_cols(gate_grad, gate_w) + contract_cols(up_grad, up_w)).astype(jnp.bfloat16)
    return comb_grad, out_grad, gate_grad, up_grad, in_grad


def pieces(array, count):
    size = array.shape[0] // count
    return [array[i * size : (i + 1) * size] for i in range(count)]


def on_device(sorted_rows, combine, cotangent, starts, w_gate, w_up, w_down):
    weights = (w_gate[0], w_up[0], w_down[0])
    count_rows = sorted_rows.shape[0]
    lead_count = jnp.remainder(starts[0], count_rows)
    lead_mask = jnp.arange(count_rows, dtype=jnp.int32) < lead_count
    scale = combine.astype(jnp.float32)
    zeros = jnp.zeros_like(scale)
    far_scale = shift(jnp.where(lead_mask, scale, zeros), -1)[:, None]
    far_rows = [shift(piece, -1) for piece in pieces(sorted_rows, X_CHUNKS)]
    far_cotan = [shift(piece, -1) for piece in pieces(cotangent, C_CHUNKS)]

    own_scale = jnp.where(lead_mask, zeros, scale)[:, None]
    gate_pre, up_pre, own_hidden, expert_out, own_mixed = forward(sorted_rows, own_scale, *weights)
    own_comb, own_outg, own_gateg, own_upg, own_ing = backward(
        cotangent, own_scale, gate_pre, up_pre, expert_out, *weights
    )

    ahead = [
        forward(rows, scale_col, *weights)
        for rows, scale_col in zip(far_rows, pieces(far_scale, X_CHUNKS))
    ]
    back_mixed = [shift(part[4], 1) for part in ahead]
    gate_pre, up_pre, hidden, expert_out = (
        jnp.concatenate([part[i] for part in ahead], axis=0) for i in range(4)
    )
    behind = [
        backward(*args, *weights)
        for args in zip(
            far_cotan,
            *(pieces(array, C_CHUNKS) for array in (far_scale, gate_pre, up_pre, expert_out)),
        )
    ]
    back_ing = [shift(part[4], 1) for part in behind]
    far_comb, far_outg, far_gateg, far_upg = (
        jnp.concatenate([part[i] for part in behind], axis=0) for i in range(4)
    )
    back_comb = shift(far_comb, 1)
    far_rows = jnp.concatenate(far_rows, axis=0)

    grad_gate = contract_rows(sorted_rows, own_gateg) + contract_rows(far_rows, far_gateg)
    grad_up = contract_rows(sorted_rows, own_upg) + contract_rows(far_rows, far_upg)
    grad_down = contract_rows(own_hidden, own_outg) + contract_rows(hidden, far_outg)
    lead_col = lead_mask[:, None]
    mixed = jnp.where(lead_col, jnp.concatenate(back_mixed, axis=0), own_mixed)
    comb_grad = jnp.where(lead_mask, back_comb, own_comb).astype(jnp.bfloat16)
    in_grad = jnp.where(lead_col, jnp.concatenate(back_ing, axis=0), own_ing)
    return (
        mixed,
        comb_grad,
        in_grad,
        grad_gate.astype(jnp.bfloat16)[None],
        grad_up.astype(jnp.bfloat16)[None],
        grad_down.astype(jnp.bfloat16)[None],
    )


def solution(mesh):
    in_specs = (
        P(AXES, None),
        P(AXES),
        P(AXES, None),
        P(AXES),
        P(AXES, None, None),
        P(AXES, None, None),
        P(AXES, None, None),
    )
    out_specs = (
        P(AXES, None),
        P(AXES),
        P(AXES, None),
        P(AXES, None, None),
        P(AXES, None, None),
        P(AXES, None, None),
    )
    return jax.shard_map(
        on_device, mesh=mesh, in_specs=in_specs, out_specs=out_specs, check_vma=False
    )
```

time: 631 us -> 110 us (0.17)
  the two profiles are of different devices: /device:TPU:96 before, /device:TPU:0 now
where the time goes in v1:
time: 110 us
  matrix products  44.9 us (41%)
  waiting for transfers between devices  30.5 us (28%)
  starting transfers between devices  17.9 us (16%)
  local copies, waits for them, and re-layouts  12.7 us (12%)
  other arithmetic  2.06 us (2%)
  between operations  1.7 us (2%)
    ppermute x14, waiting for transfers between devices, shift(): lax.ppermute(block, AXES, [(i, (i + distance) % count) for i in range(cou...  30.5 us
    dot_general x15, matrix products, contract_cols(): lax.dot_general(left, right, (((1,), (1,)), ((), ())), preferred_element_...  23.7 us
    ppermute x14, starting transfers between devices, shift(): lax.ppermute(block, AXES, [(i, (i + distance) % count) for i in range(cou...  17.9 us
    dot_general x6, matrix products, contract_rows(): lax.dot_general(left, right, (((0,), (0,)), ((), ())), preferred_element_...  11.4 us
    unnamed x15, local copies, waits for them, and re-layouts  10 us
    dot_general x3, matrix products, forward(): expert_out = jnp.dot(hidden, down_w, preferred_element_type=jnp.float32)  5.17 us
    slice x4, local copies, waits for them, and re-layouts, pieces(): return [array[i * size:(i + 1) * size] for i in range(count)]  2.6 us
    dot_general x3, matrix products, forward(): gate_pre = jnp.dot(rows_in, gate_w, preferred_element_type=jnp.float32)  2.42 us
  transfers between devices with their start and end apart: 14, of which 3 were waited for; matrix products, arithmetic and copies ran while one was open for 48% of the time, Pallas kernels for 0%

profile of v1, /device:TPU:0, one launch (start us, length us, event | category | flops | bytes accessed | tf_op | source)
XLA Modules:
  0.0 109.8 jit_solution(13564981499316519808)
XLA Ops:
  0.6 0.0 copy-start
  1.5 0.0 copy-start.3
  1.5 0.8 convert_select_fusion
  2.3 8.2 %collective-permute-start = (f32[256]{0:T(256)S(1)}, f32[256]{0:T(256)S(1)}, u32[]{:S(2)}, u32[]{:S(2)}) collective-permute-start(f32[256]{0:T(256)S(1)} %get-tuple-element.46), channel_id=1, source_target_pairs={{0,127},{1,0},{2,1},{3,2},{4,3},{5,4},{6,5},{7,6},{8,7},{9,8},{10,... | collective-permute-start | bytes 3080 | tf_op jit(solution)/shard_map/ppermute | solution.py:13
  10.5 1.3 %fusion.137 = (bf16[64,2048]{1,0:T(8,128)(2,1)S(1)}, bf16[64,2048]{1,0:T(8,128)(2,1)S(1)}, bf16[64,2048]{1,0:T(8,128)(2,1)S(1)}, bf16[64,2048]{1,0:T(8,128)(2,1)S(1)}) fusion(bf16[256,2048]{1,0:T(8,128)(2,1)} %param.9), kind=kLoop, calls=%fused_computation.157 | loop fusion | bytes 2097152 | tf_op jit(solution)/shard_map/slice | solution.py:54
  11.8 0.7 collective-permute-start.6
  12.4 0.5 collective-permute-start.7
  13.0 0.3 collective-permute-start.5
  13.2 1.3 %fusion.138 = (bf16[128,2048]{1,0:T(8,128)(2,1)S(1)}, bf16[128,2048]{1,0:T(8,128)(2,1)S(1)}) fusion(bf16[256,2048]{1,0:T(8,128)(2,1)} %param.7), kind=kLoop, calls=%fused_computation.158 | loop fusion | bytes 2097152 | tf_op jit(solution)/shard_map/slice | solution.py:54
  14.5 0.0 copy-start.1
  14.5 0.0 copy-start.4
  14.5 2.4 %collective-permute-start.1 = (bf16[128,2048]{1,0:T(8,128)(2,1)S(1)}, bf16[128,2048]{1,0:T(8,128)(2,1)S(1)}, u32[]{:S(2)}, u32[]{:S(2)}) collective-permute-start(bf16[128,2048]{1,0:T(8,128)(2,1)S(1)} %get-tuple-element.23), channel_id=1, source_target_pairs={{0,127},{1,0},{2,1},{3,2},{4,3},{5,4},{6,5},{7,6},{8,7},{9,8},{10,... | collective-permute-start | bytes 1572872 | tf_op jit(solution)/shard_map/ppermute | solution.py:13
  16.9 1.0 fusion.28
  17.9 1.0 fusion.2
  19.0 1.3 %multiply_convert_fusion.4 = (bf16[256,768]{1,0:T(8,128)(2,1)S(1)}, bf16[256,768]{1,0:T(8,128)(2,1)S(1)}, bf16[256,768]{1,0:T(8,128)(2,1)S(1)}) fusion(f32[256,768]{1,0:T(8,128)S(1)} %fusion.2, f32[256,768]{1,0:T(8,128)S(1)} %fusion.28, bf16[256,2048]{1,0:T(8,128)(2,1)S(1)} %copy-done.3, bf16[1,2048,768]{2,1,0:T(8,128)(2,1)S(1)} %copy-done), kind=kOutput, calls=%fused_computation.83 | convolution fusion | flops 808255488 | bytes 6946816 | tf_op jit(solution)/shard_map/dot_general | solution.py:29
  20.2 2.4 %fusion.83 = (bf16[256]{0:T(256)(128)(2,1)S(1)}, f32[256,2048]{1,0:T(8,128)}) fusion(bf16[256,2048]{1,0:T(8,128)(2,1)S(1)} %copy-done.4, bf16[256,768]{1,0:T(8,128)(2,1)S(1)} %get-tuple-element.18, bf16[1,768,2048]{2,1,0:T(8,128)(2,1)S(1)} %copy-done.1), kind=kOutput, calls=%fused_computation.68 | convolution fusion | flops 806878976 | bytes 6685184 | tf_op jit(solution)/shard_map/dot_general | solution.py:33
  22.6 1.1 %fusion.102 = f32[768,2048]{1,0:T(8,128)S(1)} fusion(bf16[256,768]{1,0:T(8,128)(2,1)S(1)} %get-tuple-element.18, bf16[256,2048]{1,0:T(8,128)(2,1)S(1)} %copy-done.4, f32[256]{0:T(256)S(1)} %get-tuple-element.45), kind=kOutput, calls=%fused_computation.103 | convolution fusion | flops 806879232 | bytes 7734272 | tf_op jit(solution)/shard_map/dot_general | solution.py:17
  23.7 2.4 %fusion.18 = f32[256,2048]{1,0:T(8,128)} fusion(bf16[256,768]{1,0:T(8,128)(2,1)S(1)} %get-tuple-element.17, bf16[1,2048,768]{2,1,0:T(8,128)(2,1)S(1)} %copy-done.2), kind=kOutput, calls=%fused_computation.21 | convolution fusion | flops 805306368 | bytes 5636096 | tf_op jit(solution)/shard_map/dot_general | solution.py:23
  26.1 1.0 fusion.142
  27.1 1.0 fusion.141
  28.1 0.0 collective-permute-done
  28.2 1.1 %collective-permute-start.8 = (bf16[64,2048]{1,0:T(8,128)(2,1)S(1)}, bf16[64,2048]{1,0:T(8,128)(2,1)S(1)}, u32[]{:S(2)}, u32[]{:S(2)}) collective-permute-start(bf16[64,2048]{1,0:T(8,128)(2,1)S(1)} %get-tuple-element.22), channel_id=1, source_target_pairs={{0,127},{1,0},{2,1},{3,2},{4,3},{5,4},{6,5},{7,6},{8,7},{9,8},{10,... | collective-permute-start | bytes 786440 | tf_op jit(solution)/shard_map/ppermute | solution.py:13
  29.3 0.1 fusion.139
  29.4 14.2 %collective-permute-done.1 = bf16[128,2048]{1,0:T(8,128)(2,1)S(1)} collective-permute-done((bf16[128,2048]{1,0:T(8,128)(2,1)S(1)}, bf16[128,2048]{1,0:T(8,128)(2,1)S(1)}, u32[]{:S(2)}, u32[]{:S(2)}) %collective-permute-start.1) | collective-permute-done | bytes 524320 | tf_op jit(solution)/shard_map/ppermute | solution.py:13
  43.5 4.6 %collective-permute-start.3 = (bf16[128,2048]{1,0:T(8,128)(2,1)S(1)}, bf16[128,2048]{1,0:T(8,128)(2,1)S(1)}, u32[]{:S(2)}, u32[]{:S(2)}) collective-permute-start(bf16[128,2048]{1,0:T(8,128)(2,1)S(1)} %get-tuple-element.24), channel_id=1, source_target_pairs={{0,127},{1,0},{2,1},{3,2},{4,3},{5,4},{6,5},{7,6},{8,7},{9,8},{10,... | collective-permute-start | bytes 1572872 | tf_op jit(solution)/shard_map/ppermute | solution.py:13
  48.1 0.6 fusion.48
  48.7 0.6 multiply_convert_fusion.7
  49.4 1.4 %multiply_convert_fusion.2 = (bf16[128,2048]{1,0:T(8,128)(2,1)}, f32[128,2048]{1,0:T(8,128)S(1)}) fusion(f32[128]{0:T(128)S(1)} %get-tuple-element.41, bf16[128,768]{1,0:T(8,128)(2,1)S(1)} %get-tuple-element.49, bf16[1,768,2048]{2,1,0:T(8,128)(2,1)S(1)} %copy-done.1), kind=kOutput, calls=%fused_computation.81 | convolution fusion | flops 403177472 | bytes 4915712 | tf_op jit(solution)/shard_map/dot_general | solution.py:33
  50.8 0.0 collective-permute-done.5
  50.8 0.3 fusion.94
  51.1 1.1 fusion.8
  52.2 1.1 %fusion.133 = (bf16[64,768]{1,0:T(8,128)(2,1)S(1)}, bf16[64,768]{1,0:T(8,128)(2,1)S(1)}, bf16[64,768]{1,0:T(8,128)(2,1)S(1)}, bf16[64,768]{1,0:T(8,128)(2,1)S(1)}) fusion(f32[128,768]{1,0:T(8,128)S(1)} %get-tuple-element.50, f32[128,768]{1,0:T(8,128)S(1)} %fusion.48, f32[64,768]{1,0:T(8,128)S(1)} %fusion.8, bf16[64,2048]{1,0:T(8,128)(2,1)S(1)} %get-tuple-element.33, ...), kind=kOutput, calls=%fused_computation.138 | convolution fusion | flops 202604544 | bytes 4784128 | tf_op jit(solution)/shard_map/dot_general | solution.py:23
  53.3 1.1 fusion.24
  54.4 1.1 fusion.77
  55.5 0.1 collective-permute-start.11
  55.6 1.1 fusion.26
  56.6 1.8 %fusion.80 = bf16[64,2048]{1,0:T(8,128)(2,1)} fusion(f32[64,2048]{1,0:T(8,128)S(1)} %fusion.26, bf16[64,768]{1,0:T(8,128)(2,1)S(1)} %get-tuple-element.25, bf16[1,2048,768]{2,1,0:T(8,128)(2,1)S(1)} %copy-done), kind=kOutput, calls=%fused_computation.67 | convolution fusion | flops 201588736 | bytes 4030464 | tf_op jit(solution)/shard_map/dot_general | solution.py:23
  58.4 0.0 collective-permute-start.10
  58.4 0.0 collective-permute-done.3
  58.4 0.0 collective-permute-start.2
  58.4 0.6 fusion.46
  59.0 0.6 multiply_convert_fusion.6
  59.6 1.4 %multiply_convert_fusion.1 = (bf16[128,2048]{1,0:T(8,128)(2,1)}, f32[128,2048]{1,0:T(8,128)S(1)}) fusion(f32[128]{0:T(128)S(1)} %get-tuple-element.42, bf16[128,768]{1,0:T(8,128)(2,1)S(1)} %get-tuple-element.47, bf16[1,768,2048]{2,1,0:T(8,128)(2,1)S(1)} %copy-done.1), kind=kOutput, calls=%fused_computation.80 | convolution fusion | flops 403177472 | bytes 4915712 | tf_op jit(solution)/shard_map/dot_general | solution.py:33
  61.0 0.0 collective-permute-done.8
  61.1 0.3 fusion.98
  61.4 0.1 pad_maximum_fusion
  61.5 0.0 collective-permute-start.9
  61.5 1.1 fusion.4
  62.6 1.1 %fusion.127 = (bf16[64,768]{1,0:T(8,128)(2,1)S(1)}, bf16[64,768]{1,0:T(8,128)(2,1)S(1)}, bf16[64,768]{1,0:T(8,128)(2,1)S(1)}, bf16[64,768]{1,0:T(8,128)(2,1)S(1)}) fusion(f32[128,768]{1,0:T(8,128)S(1)} %get-tuple-element.48, f32[128,768]{1,0:T(8,128)S(1)} %fusion.46, f32[64,768]{1,0:T(8,128)S(1)} %fusion.4, bf16[64,2048]{1,0:T(8,128)(2,1)S(1)} %get-tuple-element.35, ...), kind=kOutput, calls=%fused_computation.130 | convolution fusion | flops 202604544 | bytes 4784128 | tf_op jit(solution)/shard_map/dot_general | solution.py:23
  63.7 1.1 fusion.20
  64.8 1.8 %fusion.71 = bf16[64,2048]{1,0:T(8,128)(2,1)} fusion(f32[64,2048]{1,0:T(8,128)S(1)} %fusion.20, bf16[64,768]{1,0:T(8,128)(2,1)S(1)} %get-tuple-element.28, bf16[1,2048,768]{2,1,0:T(8,128)(2,1)S(1)} %copy-done), kind=kOutput, calls=%fused_computation.64 | convolution fusion | flops 201588736 | bytes 4030464 | tf_op jit(solution)/shard_map/dot_general | solution.py:23
  66.6 0.0 collective-permute-start.13
  66.6 1.1 fusion.22
  67.6 2.7 %fusion.50 = bf16[1,768,2048]{2,1,0:T(8,128)(2,1)} fusion(f32[768,2048]{1,0:T(8,128)S(1)} %fusion.102, bf16[64,2048]{1,0:T(8,128)(2,1)S(1)} %get-tuple-element.36, bf16[64,2048]{1,0:T(8,128)(2,1)S(1)} %get-tuple-element.35, bf16[64,2048]{1,0:T(8,128)(2,1)S(1)} %get-tuple-element.34, bf16[64,2048]{1,0:T(8,128)(2,1)S(1)} %get-tuple-element.33, ...), kind=kOutput, calls=%fused_computation.53 | convolution fusion | flops 813432832 | bytes 10878976 | tf_op jit(solution)/shard_map/dot_general | solution.py:17
  70.4 2.8 %fusion.51 = bf16[1,2048,768]{1,2,0:T(8,128)(2,1)} fusion(bf16[256,2048]{1,0:T(8,128)(2,1)S(1)} %constant_dynamic-update-slice_fusion, f32[768,2048]{1,0:T(8,128)S(1)} %fusion.141, bf16[64,768]{1,0:T(8,128)(2,1)S(1)} %get-tuple-element.28, bf16[64,768]{1,0:T(8,128)(2,1)S(1)} %get-tuple-element.27, bf16[64,768]{1,0:T(8,128)(2,1)S(1)} %get-tuple-element.26, ...), kind=kOutput, calls=%fused_computation.54 | convolution fusion | flops 810024960 | bytes 10878976 | tf_op jit(solution)/shard_map/dot_general | solution.py:17
  73.2 1.8 %fusion.74 = bf16[64,2048]{1,0:T(8,128)(2,1)} fusion(f32[64,2048]{1,0:T(8,128)S(1)} %fusion.22, bf16[64,768]{1,0:T(8,128)(2,1)S(1)} %get-tuple-element.27, bf16[1,2048,768]{2,1,0:T(8,128)(2,1)S(1)} %copy-done), kind=kOutput, calls=%fused_computation.65 | convolution fusion | flops 201588736 | bytes 4030464 | tf_op jit(solution)/shard_map/dot_general | solution.py:23
  74.9 11.5 %collective-permute-done.9 = bf16[256]{0:T(256)(128)(2,1)S(1)} collective-permute-done((bf16[256]{0:T(256)(128)(2,1)S(1)}, bf16[256]{0:T(256)(128)(2,1)S(1)}, u32[]{:S(2)}, u32[]{:S(2)}) %collective-permute-start.9) | collective-permute-done | bytes 544 | tf_op jit(solution)/shard_map/ppermute | solution.py:13
  86.5 0.7 copy-done.5
  87.2 2.8 %fusion.52 = bf16[1,2048,768]{1,2,0:T(8,128)(2,1)} fusion(bf16[256,2048]{1,0:T(8,128)(2,1)S(1)} %constant_dynamic-update-slice_fusion, f32[768,2048]{1,0:T(8,128)S(1)} %fusion.142, bf16[64,768]{1,0:T(8,128)(2,1)S(1)} %get-tuple-element.29, bf16[64,768]{1,0:T(8,128)(2,1)S(1)} %get-tuple-element.32, bf16[64,768]{1,0:T(8,128)(2,1)S(1)} %get-tuple-element.30, ...), kind=kOutput, calls=%fused_computation.55 | convolution fusion | flops 810024960 | bytes 10878976 | tf_op jit(solution)/shard_map/dot_general | solution.py:17
  89.9 4.6 %copy.15 = bf16[1,2048,768]{2,1,0:T(8,128)(2,1)} copy(bf16[1,2048,768]{1,2,0:T(8,128)(2,1)} %fusion.51) | data formatting | bytes 6291456
  94.6 4.6 %copy.16 = bf16[1,2048,768]{2,1,0:T(8,128)(2,1)} copy(bf16[1,2048,768]{1,2,0:T(8,128)(2,1)} %fusion.52) | data formatting | bytes 6291456
  99.2 0.5 select_convert_fusion
  99.7 4.8 %collective-permute-done.4 = bf16[128,2048]{1,0:T(8,128)(2,1)} collective-permute-done((bf16[128,2048]{1,0:T(8,128)(2,1)}, bf16[128,2048]{1,0:T(8,128)(2,1)}, u32[]{:S(2)}, u32[]{:S(2)}) %collective-permute-start.4) | collective-permute-done | bytes 524320 | tf_op jit(solution)/shard_map/ppermute | solution.py:13
  104.5 5.2 %maximum_select_fusion = (bf16[256,2048]{1,0:T(8,128)(2,1)}, bf16[256,2048]{1,0:T(8,128)(2,1)}) fusion(bf16[64,2048]{1,0:T(8,128)(2,1)} %collective-permute-done.13, bf16[64,2048]{1,0:T(8,128)(2,1)} %collective-permute-done.12, bf16[64,2048]{1,0:T(8,128)(2,1)} %copy-done.5, bf16[64,2048]{1,0:T(8,128)(2,1)} %collective-permute-done.10, ...), kind=kOutput, calls=%fused_computation.72 | convolution fusion | flops 814743552 | bytes 11928832 | tf_op jit(solution)/shard_map/dot_general | solution.py:23
  (20 shorter events, 0.1 us)
Async XLA Ops:
  0.6 18.3 %copy-start = (bf16[1,2048,768]{2,1,0:T(8,128)(2,1)S(1)}, bf16[1,2048,768]{2,1,0:T(8,128)(2,1)}, u32[]{:S(2)}) copy-start(bf16[1,2048,768]{2,1,0:T(8,128)(2,1)} %param.11) | copy-start | bytes 9437188
  1.5 15.5 %copy-start.2 = (bf16[1,2048,768]{2,1,0:T(8,128)(2,1)S(1)}, bf16[1,2048,768]{2,1,0:T(8,128)(2,1)}, u32[]{:S(2)}) copy-start(bf16[1,2048,768]{2,1,0:T(8,128)(2,1)} %param.12) | copy-start | bytes 9437188
  1.5 15.5 %copy-start.3 = (bf16[256,2048]{1,0:T(8,128)(2,1)S(1)}, bf16[256,2048]{1,0:T(8,128)(2,1)}, u32[]{:S(2)}) copy-start(bf16[256,2048]{1,0:T(8,128)(2,1)} %param.7) | copy-start | bytes 3145732
  2.3 25.9 %collective-permute-start = (f32[256]{0:T(256)S(1)}, f32[256]{0:T(256)S(1)}, u32[]{:S(2)}, u32[]{:S(2)}) collective-permute-start(f32[256]{0:T(256)S(1)} %get-tuple-element.46), channel_id=1, source_target_pairs={{0,127},{1,0},{2,1},{3,2},{4,3},{5,4},{6,5},{7,6},{8,7},{9,8},{10,... | collective-permute-start | bytes 3080 | tf_op jit(solution)/shard_map/ppermute | solution.py:13
  11.8 39.0 %collective-permute-start.6 = (bf16[64,2048]{1,0:T(8,128)(2,1)S(1)}, bf16[64,2048]{1,0:T(8,128)(2,1)S(1)}, u32[]{:S(2)}, u32[]{:S(2)}) collective-permute-start(bf16[64,2048]{1,0:T(8,128)(2,1)S(1)} %get-tuple-element.19), channel_id=1, source_target_pairs={{0,127},{1,0},{2,1},{3,2},{4,3},{5,4},{6,5},{7,6},{8,7},{9,8},{10,... | collective-permute-start | bytes 786440 | tf_op jit(solution)/shard_map/ppermute | solution.py:13
  12.4 48.6 %collective-permute-start.7 = (bf16[64,2048]{1,0:T(8,128)(2,1)S(1)}, bf16[64,2048]{1,0:T(8,128)(2,1)S(1)}, u32[]{:S(2)}, u32[]{:S(2)}) collective-permute-start(bf16[64,2048]{1,0:T(8,128)(2,1)S(1)} %get-tuple-element.20), channel_id=1, source_target_pairs={{0,127},{1,0},{2,1},{3,2},{4,3},{5,4},{6,5},{7,6},{8,7},{9,8},{10,... | collective-permute-start | bytes 786440 | tf_op jit(solution)/shard_map/ppermute | solution.py:13
  13.0 37.8 %collective-permute-start.5 = (bf16[64,2048]{1,0:T(8,128)(2,1)S(1)}, bf16[64,2048]{1,0:T(8,128)(2,1)S(1)}, u32[]{:S(2)}, u32[]{:S(2)}) collective-permute-start(bf16[64,2048]{1,0:T(8,128)(2,1)S(1)} %get-tuple-element.21), channel_id=1, source_target_pairs={{0,127},{1,0},{2,1},{3,2},{4,3},{5,4},{6,5},{7,6},{8,7},{9,8},{10,... | collective-permute-start | bytes 786440 | tf_op jit(solution)/shard_map/ppermute | solution.py:13
  14.5 3.4 %copy-start.1 = (bf16[1,768,2048]{2,1,0:T(8,128)(2,1)S(1)}, bf16[1,768,2048]{2,1,0:T(8,128)(2,1)}, u32[]{:S(2)}) copy-start(bf16[1,768,2048]{2,1,0:T(8,128)(2,1)} %param.13) | copy-start | bytes 9437188
  14.5 3.4 %copy-start.4 = (bf16[256,2048]{1,0:T(8,128)(2,1)S(1)}, bf16[256,2048]{1,0:T(8,128)(2,1)}, u32[]{:S(2)}) copy-start(bf16[256,2048]{1,0:T(8,128)(2,1)} %param.9) | copy-start | bytes 3145732
  14.5 29.0 %collective-permute-start.1 = (bf16[128,2048]{1,0:T(8,128)(2,1)S(1)}, bf16[128,2048]{1,0:T(8,128)(2,1)S(1)}, u32[]{:S(2)}, u32[]{:S(2)}) collective-permute-start(bf16[128,2048]{1,0:T(8,128)(2,1)S(1)} %get-tuple-element.23), channel_id=1, source_target_pairs={{0,127},{1,0},{2,1},{3,2},{4,3},{5,4},{6,5},{7,6},{8,7},{9,8},{10,... | collective-permute-start | bytes 1572872 | tf_op jit(solution)/shard_map/ppermute | solution.py:13
  28.2 32.9 %collective-permute-start.8 = (bf16[64,2048]{1,0:T(8,128)(2,1)S(1)}, bf16[64,2048]{1,0:T(8,128)(2,1)S(1)}, u32[]{:S(2)}, u32[]{:S(2)}) collective-permute-start(bf16[64,2048]{1,0:T(8,128)(2,1)S(1)} %get-tuple-element.22), channel_id=1, source_target_pairs={{0,127},{1,0},{2,1},{3,2},{4,3},{5,4},{6,5},{7,6},{8,7},{9,8},{10,... | collective-permute-start | bytes 786440 | tf_op jit(solution)/shard_map/ppermute | solution.py:13
  43.5 14.9 %collective-permute-start.3 = (bf16[128,2048]{1,0:T(8,128)(2,1)S(1)}, bf16[128,2048]{1,0:T(8,128)(2,1)S(1)}, u32[]{:S(2)}, u32[]{:S(2)}) collective-permute-start(bf16[128,2048]{1,0:T(8,128)(2,1)S(1)} %get-tuple-element.24), channel_id=1, source_target_pairs={{0,127},{1,0},{2,1},{3,2},{4,3},{5,4},{6,5},{7,6},{8,7},{9,8},{10,... | collective-permute-start | bytes 1572872 | tf_op jit(solution)/shard_map/ppermute | solution.py:13
  55.5 31.0 %collective-permute-start.11 = (bf16[64,2048]{1,0:T(8,128)(2,1)S(1)}, bf16[64,2048]{1,0:T(8,128)(2,1)S(1)}, u32[]{:S(2)}, u32[]{:S(2)}) collective-permute-start(bf16[64,2048]{1,0:T(8,128)(2,1)S(1)} %fusion.77), channel_id=1, source_target_pairs={{0,1},{1,2},{2,3},{3,4},{4,5},{5,6},{6,7},{7,8},{8,9},{9,10},{10,1... | collective-permute-start | bytes 786440 | tf_op jit(solution)/shard_map/ppermute | solution.py:13
  58.4 41.3 %collective-permute-start.10 = (bf16[64,2048]{1,0:T(8,128)(2,1)}, bf16[64,2048]{1,0:T(8,128)(2,1)}, u32[]{:S(2)}, u32[]{:S(2)}) collective-permute-start(bf16[64,2048]{1,0:T(8,128)(2,1)} %fusion.80), channel_id=1, source_target_pairs={{0,1},{1,2},{2,3},{3,4},{4,5},{5,6},{6,7},{7,8},{8,9},{9,10},{10,1... | collective-permute-start | bytes 786440 | tf_op jit(solution)/shard_map/ppermute | solution.py:13
  58.4 41.3 %collective-permute-start.2 = (bf16[128,2048]{1,0:T(8,128)(2,1)}, bf16[128,2048]{1,0:T(8,128)(2,1)}, u32[]{:S(2)}, u32[]{:S(2)}) collective-permute-start(bf16[128,2048]{1,0:T(8,128)(2,1)} %get-tuple-element.53), channel_id=1, source_target_pairs={{0,1},{1,2},{2,3},{3,4},{4,5},{5,6},{6,7},{7,8},{8,9},{9,10},{10,1... | collective-permute-start | bytes 1572872 | tf_op jit(solution)/shard_map/ppermute | solution.py:13
  61.5 25.0 %collective-permute-start.9 = (bf16[256]{0:T(256)(128)(2,1)S(1)}, bf16[256]{0:T(256)(128)(2,1)S(1)}, u32[]{:S(2)}, u32[]{:S(2)}) collective-permute-start(bf16[256]{0:T(256)(128)(2,1)S(1)} %pad_maximum_fusion), channel_id=1, source_target_pairs={{0,1},{1,2},{2,3},{3,4},{4,5},{5,6},{6,7},{7,8},{8,9},{9,10},{10,1... | collective-permute-start | bytes 1544 | tf_op jit(solution)/shard_map/ppermute | solution.py:13
  66.6 33.1 %collective-permute-start.13 = (bf16[64,2048]{1,0:T(8,128)(2,1)}, bf16[64,2048]{1,0:T(8,128)(2,1)}, u32[]{:S(2)}, u32[]{:S(2)}) collective-permute-start(bf16[64,2048]{1,0:T(8,128)(2,1)} %fusion.71), channel_id=1, source_target_pairs={{0,1},{1,2},{2,3},{3,4},{4,5},{5,6},{6,7},{7,8},{8,9},{9,10},{10,1... | collective-permute-start | bytes 786440 | tf_op jit(solution)/shard_map/ppermute | solution.py:13
  86.5 13.2 %collective-permute-start.12 = (bf16[64,2048]{1,0:T(8,128)(2,1)}, bf16[64,2048]{1,0:T(8,128)(2,1)}, u32[]{:S(2)}, u32[]{:S(2)}) collective-permute-start(bf16[64,2048]{1,0:T(8,128)(2,1)} %fusion.74), channel_id=1, source_target_pairs={{0,1},{1,2},{2,3},{3,4},{4,5},{5,6},{6,7},{7,8},{8,9},{9,10},{10,1... | collective-permute-start | bytes 786440 | tf_op jit(solution)/shard_map/ppermute | solution.py:13
  86.5 0.7 copy-start.5
  87.2 17.4 %collective-permute-start.4 = (bf16[128,2048]{1,0:T(8,128)(2,1)}, bf16[128,2048]{1,0:T(8,128)(2,1)}, u32[]{:S(2)}, u32[]{:S(2)}) collective-permute-start(bf16[128,2048]{1,0:T(8,128)(2,1)} %get-tuple-element.51), channel_id=1, source_target_pairs={{0,1},{1,2},{2,3},{3,4},{4,5},{5,6},{6,7},{7,8},{8,9},{9,10},{10,1... | collective-permute-start | bytes 1572872 | tf_op jit(solution)/shard_map/ppermute | solution.py:13

commit v2 on v0

v2 whole, which is shorter than its diff:
```python
import functools

import jax
import jax.numpy as jnp
from jax import lax
from jax.experimental import pallas as pl
from jax.experimental.pallas import tpu as pltpu
from jax.sharding import PartitionSpec as P

AXES = ("rows", "grp")
MESH = pl.DeviceIdType.MESH
F32 = jnp.float32
BF16 = jnp.bfloat16
X_CHUNKS = (64, 64, 64, 64)
C_CHUNKS = (64, 64, 64, 64)
HT = 256
DT = 512


def spans(sizes):
    start, out = 0, []
    for size in sizes:
        out.append((start, size))
        start += size
    return out


def dot(left, right):
    return jnp.dot(left, right, preferred_element_type=F32)


def dot_cols(left, right):
    return lax.dot_general(left, right, (((1,), (1,)), ((), ())), preferred_element_type=F32)


def dot_rows(left, right):
    return lax.dot_general(left, right, (((0,), (0,)), ((), ())), preferred_element_type=F32)


def tile(step, width):
    return pl.ds(pl.multiple_of(step * width, width), width)


def to_column(row_block):
    count = row_block.shape[1]
    return jnp.broadcast_to(row_block[0:1, :], (128, count)).T


def to_row(column, rows):
    return jnp.broadcast_to(column, (column.shape[0], 128)).T[0:rows, :]


def exchange_kernel(
    sizes,
    x_hbm, cot_hbm, own_scale, lead_scale, wg_hbm, wu_hbm, wd_hbm,
    own_mixed_o, own_ing_o, back_mixed_o, back_ing_o, own_comb_o, back_comb_o,
    far_x_o, hid_o, gg_o, ug_o, og_o,
    wg, wu, wd, x, cot, far_x, far_cot, far_scale, own_col, far_col,
    gate, up, far_gate, far_up, far_out, hid, gg, ug, og,
    own_mixed, own_ing, send_mixed, send_ing, far_comb, comb_row,
    load_sem, store_sem, scale_sem, x_sem, c_sem, m_sem, i_sem, comb_sem,
):
    n_rows, n_grp = sizes
    count = x.shape[0]
    d_tiles, h_tiles = x.shape[1] // DT, gate.shape[1] // HT
    row, col = lax.axis_index("rows"), lax.axis_index("grp")
    me = row * n_grp + col
    left = lax.rem(me + n_rows * n_grp - 1, n_rows * n_grp)
    right = lax.rem(me + 1, n_rows * n_grp)
    left_id = (left // n_grp, lax.rem(left, n_grp))
    right_id = (right // n_grp, lax.rem(right, n_grp))

    loads = [
        pltpu.make_async_copy(src, dst, load_sem.at[i])
        for i, (src, dst) in enumerate(
            ((wg_hbm, wg), (wu_hbm, wu), (wd_hbm, wd), (x_hbm, x), (cot_hbm, cot))
        )
    ]
    for load in loads:
        load.start()

    barrier = pltpu.get_barrier_semaphore()
    for peer in (left_id, right_id):
        pl.semaphore_signal(barrier, inc=1, device_id=peer, device_id_type=MESH)
    pl.semaphore_wait(barrier, 2)

    def remote(src, dst, sems, index, peer):
        return pltpu.make_async_remote_copy(
            src_ref=src,
            dst_ref=dst,
            send_sem=sems.at[0, index],
            recv_sem=sems.at[1, index],
            device_id=peer,
            device_id_type=MESH,
        )

    scale_copy = remote(lead_scale, far_scale, scale_sem, 0, left_id)
    scale_copy.start()
    x_copies, c_copies = [], []
    for i, (lo, size) in enumerate(spans(X_CHUNKS)):
        at = pl.ds(lo, size)
        x_copies.append(remote(x_hbm.at[at], far_x.at[at], x_sem, i, left_id))
        x_copies[-1].start()
    for i, (lo, size) in enumerate(spans(C_CHUNKS)):
        at = pl.ds(lo, size)
        c_copies.append(remote(cot_hbm.at[at], far_cot.at[at], c_sem, i, left_id))
        c_copies[-1].start()

    own_col[...] = to_column(own_scale[...])
    scale_copy.wait()
    far_col[...] = to_column(far_scale[...])
    loads[0].wait()
    loads[1].wait()
    loads[2].wait()

    def gate_up(rows_ref, at, gate_ref, up_ref, hid_at):
        @pl.loop(0, h_tiles)
        def _(step):
            cols = tile(step, HT)
            rows = rows_ref[at, :]
            g = dot(rows, wg[:, cols])
            u = dot(rows, wu[:, cols])
            gate_ref[at, cols] = g
            up_ref[at, cols] = u
            hid[hid_at, cols] = (g * jax.nn.sigmoid(g) * u).astype(BF16)

    def hidden_grads(og_at, act_at, gate_ref, up_ref):
        @pl.loop(0, h_tiles)
        def _(step):
            cols = tile(step, HT)
            hg = dot_cols(og[og_at, :], wd[cols, :])
            g, u = gate_ref[act_at, cols], up_ref[act_at, cols]
            s = jax.nn.sigmoid(g)
            gg[og_at, cols] = (hg * u * s * (1.0 + g * (1.0 - s))).astype(BF16)
            ug[og_at, cols] = (hg * (g * s)).astype(BF16)

    def input_grads(og_at, out_ref, out_at):
        @pl.loop(0, d_tiles)
        def _(step):
            cols = tile(step, DT)
            total = dot_cols(gg[og_at, :], wg[cols, :]) + dot_cols(ug[og_at, :], wu[cols, :])
            out_ref[out_at, cols] = total.astype(BF16)

    def far_forward(lo, size):
        at, hid_at = pl.ds(lo, size), pl.ds(count + lo, size)
        gate_up(far_x, at, far_gate, far_up, hid_at)

        @pl.loop(0, d_tiles)
        def _(step):
            cols = tile(step, DT)
            out = dot(hid[hid_at, :], wd[:, cols])
            far_out[at, cols] = out
            send_mixed[at, cols] = (far_col[at, 0:1] * out).astype(BF16)

    def far_backward(lo, size):
        at, og_at = pl.ds(lo, size), pl.ds(count + lo, size)

        def body(step, total):
            cols = tile(step, DT)
            c = far_cot[at, cols].astype(F32)
            og[og_at, cols] = (far_col[at, 0:1] * c).astype(BF16)
            return total + jnp.sum(far_out[at, cols] * c, axis=1, keepdims=True)

        total = lax.fori_loop(0, d_tiles, body, jnp.zeros((size, 1), F32))
        far_comb[at, :] = jnp.broadcast_to(total, (size, 128))
        hidden_grads(og_at, at, far_gate, far_up)
        input_grads(og_at, send_ing, at)

    own = pl.ds(0, count)

    def own_gate_up():
        loads[3].wait()
        gate_up(x, own, gate, up, own)

    def own_down():
        loads[4].wait()

        def body(step, total):
            cols = tile(step, DT)
            out = dot(hid[own, :], wd[:, cols])
            own_mixed[:, cols] = (own_col[:, 0:1] * out).astype(BF16)
            c = cot[:, cols].astype(F32)
            og[own, cols] = (own_col[:, 0:1] * c).astype(BF16)
            return total + jnp.sum(out * c, axis=1, keepdims=True)

        total = lax.fori_loop(0, d_tiles, body, jnp.zeros((count, 1), F32))
        own_comb_o[...] = to_row(total, own_comb_o.shape[0])

    stores = []

    def store(src, dst):
        stores.append(pltpu.make_async_copy(src, dst, store_sem.at[len(stores)]))
        stores[-1].start()

    def own_hidden_grads():
        store(own_mixed, own_mixed_o)
        hidden_grads(own, own, gate, up)

    def own_input_grads():
        input_grads(own, own_ing, own)
        store(own_ing, own_ing_o)

    own_steps = [own_gate_up, own_down, own_hidden_grads, own_input_grads]
    m_copies, i_copies = [], []
    for i, (lo, size) in enumerate(spans(X_CHUNKS)):
        x_copies[i].wait_recv()
        far_forward(lo, size)
        at = pl.ds(lo, size)
        m_copies.append(remote(send_mixed.at[at], back_mixed_o.at[at], m_sem, i, right_id))
        m_copies[-1].start()
        if own_steps:
            own_steps.pop(0)()
    store(far_x, far_x_o)
    store(hid, hid_o)
    for i, (lo, size) in enumerate(spans(C_CHUNKS)):
        c_copies[i].wait_recv()
        far_backward(lo, size)
        at = pl.ds(lo, size)
        i_copies.append(remote(send_ing.at[at], back_ing_o.at[at], i_sem, i, right_id))
        i_copies[-1].start()
        if own_steps:
            own_steps.pop(0)()
    for src, dst in ((gg, gg_o), (ug, ug_o), (og, og_o)):
        store(src, dst)
    comb_row[...] = far_comb[...].T[0 : comb_row.shape[0], :]
    comb_copy = remote(comb_row, back_comb_o, comb_sem, 0, right_id)
    comb_copy.start()
    for copy in stores:
        copy.wait()
    for copy in x_copies + c_copies:
        copy.wait_send()
    for copy in m_copies + i_copies:
        copy.wait()
    comb_copy.wait()


def exchange(sizes, x, cot, own_scale, lead_scale, wg, wu, wd):
    count, d = x.shape
    h = wg.shape[1]
    big = jax.ShapeDtypeStruct((count, d), BF16)
    small = jax.ShapeDtypeStruct((8, count), F32)
    act = jax.ShapeDtypeStruct((2 * count, h), BF16)
    anywhere = pl.BlockSpec(memory_space=pl.ANY)
    vmem = pl.BlockSpec(memory_space=pltpu.VMEM)
    dma = pltpu.SemaphoreType.DMA
    return pl.pallas_call(
        functools.partial(exchange_kernel, sizes),
        name="exchange",
        out_shape=(big, big, big, big, small, small, big, act, act, act,
                   jax.ShapeDtypeStruct((2 * count, d), BF16)),
        in_specs=[anywhere, anywhere, vmem, vmem, anywhere, anywhere, anywhere],
        out_specs=(anywhere,) * 4 + (vmem, anywhere) + (anywhere,) * 5,
        scratch_shapes=[
            pltpu.VMEM((d, h), BF16),
            pltpu.VMEM((d, h), BF16),
            pltpu.VMEM((h, d), BF16),
            pltpu.VMEM((count, d), BF16),
            pltpu.VMEM((count, d), BF16),
            pltpu.VMEM((count, d), BF16),
            pltpu.VMEM((count, d), BF16),
            pltpu.VMEM((8, count), F32),
            pltpu.VMEM((count, 128), F32),
            pltpu.VMEM((count, 128), F32),
            pltpu.VMEM((count, h), F32),
            pltpu.VMEM((count, h), F32),
            pltpu.VMEM((count, h), F32),
            pltpu.VMEM((count, h), F32),
            pltpu.VMEM((count, d), F32),
            pltpu.VMEM((2 * count, h), BF16),
            pltpu.VMEM((2 * count, h), BF16),
            pltpu.VMEM((2 * count, h), BF16),
            pltpu.VMEM((2 * count, d), BF16),
            pltpu.VMEM((count, d), BF16),
            pltpu.VMEM((count, d), BF16),
            pltpu.VMEM((count, d), BF16),
            pltpu.VMEM((count, d), BF16),
            pltpu.VMEM((count, 128), F32),
            pltpu.VMEM((8, count), F32),
            dma((5,)),
            dma((7,)),
            dma((2, 1)),
            dma((2, len(X_CHUNKS))),
            dma((2, len(C_CHUNKS))),
            dma((2, len(X_CHUNKS))),
            dma((2, len(C_CHUNKS))),
            dma((2, 1)),
        ],
        compiler_params=pltpu.CompilerParams(
            collective_id=0, has_side_effects=True, vmem_limit_bytes=48 * 2**20
        ),
    )(x, cot, own_scale, lead_scale, wg, wu, wd)


def finish_kernel(
    lead_ref, x, far_x, hid, gg, ug, og, own_mixed, own_ing, back_mixed, back_ing,
    grad_gate, grad_up, grad_down, mixed, ing,
):
    count = x.shape[0]
    own, far = pl.ds(0, count), pl.ds(count, count)
    grad_gate[0] = (dot_rows(x[...], gg[own, :]) + dot_rows(far_x[...], gg[far, :])).astype(BF16)
    grad_up[0] = (dot_rows(x[...], ug[own, :]) + dot_rows(far_x[...], ug[far, :])).astype(BF16)
    grad_down[0] = dot_rows(hid[...], og[...]).astype(BF16)
    lead = lax.broadcasted_iota(jnp.int32, mixed.shape, 0) < lead_ref[0]
    mixed[...] = jnp.where(lead, back_mixed[...], own_mixed[...])
    ing[...] = jnp.where(lead, back_ing[...], own_ing[...])


def finish(lead_count, x, far_x, hid, gg, ug, og, own_mixed, own_ing, back_mixed, back_ing):
    count, d = x.shape
    h = hid.shape[1]
    width = 256
    cols = pl.BlockSpec((count, width), lambda i, lead: (0, i))
    both = pl.BlockSpec((2 * count, width), lambda i, lead: (0, i))
    act = pl.BlockSpec((2 * count, h), lambda i, lead: (0, 0))
    tall = pl.BlockSpec((1, width, h), lambda i, lead: (0, i, 0))
    wide = pl.BlockSpec((1, h, width), lambda i, lead: (0, 0, i))
    return pl.pallas_call(
        finish_kernel,
        name="finish",
        out_shape=(
            jax.ShapeDtypeStruct((1, d, h), BF16),
            jax.ShapeDtypeStruct((1, d, h), BF16),
            jax.ShapeDtypeStruct((1, h, d), BF16),
            jax.ShapeDtypeStruct((count, d), BF16),
            jax.ShapeDtypeStruct((count, d), BF16),
        ),
        grid_spec=pltpu.PrefetchScalarGridSpec(
            num_scalar_prefetch=1,
            grid=(d // width,),
            in_specs=[cols, cols, act, act, act, both, cols, cols, cols, cols],
            out_specs=(tall, tall, wide, cols, cols),
        ),
        compiler_params=pltpu.CompilerParams(vmem_limit_bytes=32 * 2**20),
    )(lead_count, x, far_x, hid, gg, ug, og, own_mixed, own_ing, back_mixed, back_ing)


def solution(mesh):
    sizes = tuple(mesh.shape[axis] for axis in AXES)

    def on_device(sorted_rows, combine, cotangent, starts, w_gate, w_up, w_down):
        count = sorted_rows.shape[0]
        lead_count = jnp.remainder(starts, count)
        lead = jnp.arange(count, dtype=jnp.int32) < lead_count[0]
        scale = combine.astype(F32)
        zeros = jnp.zeros_like(scale)
        own_scale = jnp.broadcast_to(jnp.where(lead, zeros, scale), (8, count))
        lead_scale = jnp.broadcast_to(jnp.where(lead, scale, zeros), (8, count))
        (own_mixed, own_ing, back_mixed, back_ing, own_comb, back_comb, far_x, hid, gg, ug, og) = exchange(
            sizes, sorted_rows, cotangent, own_scale, lead_scale, w_gate[0], w_up[0], w_down[0]
        )
        grad_gate, grad_up, grad_down, mixed, ing = finish(
            lead_count, sorted_rows, far_x, hid, gg, ug, og, own_mixed, own_ing, back_mixed, back_ing
        )
        comb_grad = jnp.where(lead, back_comb[0], own_comb[0]).astype(BF16)
        return mixed, comb_grad, ing, grad_gate, grad_up, grad_down

    rows2, rows1, rows3 = P(AXES, None), P(AXES), P(AXES, None, None)
    return jax.shard_map(
        on_device,
        mesh=mesh,
        in_specs=(rows2, rows1, rows2, rows1, rows3, rows3, rows3),
        out_specs=(rows2, rows1, rows2, rows3, rows3, rows3),
        check_vma=False,
    )
```

time: 631 us -> 86.8 us (0.14)
  the two profiles are of different devices: /device:TPU:96 before, /device:TPU:0 now
where the time goes in v2:
time: 86.8 us; the launch traced here: 86.6 us
  Pallas kernels  80 us (92%)
  local copies, waits for them, and re-layouts  4.05 us (5%)
  between operations  1.32 us (2%)
  other arithmetic  1.18 us (1%)
    pallas_call x1, Pallas kernels, exchange(): pl.pallas_call(functools.partial(exchange_kernel, sizes), name='exchange'...  71.1 us
    pallas_call x1, Pallas kernels, finish(): pl.pallas_call(finish_kernel, name='finish', out_shape=(jax.ShapeDtypeStr...  8.91 us
    unnamed x8, local copies, waits for them, and re-layouts  4.04 us

profile of v2, /device:TPU:0, one launch (start us, length us, event | category | flops | bytes accessed | tf_op | source)
XLA Modules:
  0.0 86.6 jit_solution(1399934690347125751)
XLA Ops:
  1.3 0.7 convert_select_fusion
  2.0 0.0 copy-start
  2.0 71.1 %exchange.1 = (bf16[256,2048]{1,0:T(8,128)(2,1)S(1)}, bf16[256,2048]{1,0:T(8,128)(2,1)S(1)}, bf16[256,2048]{1,0:T(8,128)(2,1)S(1)}, bf16[256,2048]{1,0:T(8,128)(...) custom-call(bf16[256,2048]{1,0:T(8,128)(2,1)} %x.1, ...), custom_call_target="tpu_custom_call" | custom-call | tf_op jit(solution)/shard_map/exchange/pallas_call | solution.py:246
  73.1 0.5 select_convert_fusion
  73.6 0.0 copy-done
  73.6 0.0 copy-start.1
  73.6 1.6 %copy-done.1 = bf16[512,2048]{1,0:T(8,128)(2,1)S(1)} copy-done((bf16[512,2048]{1,0:T(8,128)(2,1)S(1)}, bf16[512,2048]{1,0:T(8,128)(2,1)}, u32[]{:S(2)}) %copy-start.1) | copy-done | bytes 2097176
  75.2 0.0 copy-start.2
  75.2 1.2 %copy-done.2 = bf16[256,2048]{1,0:T(8,128)(2,1)S(1)} copy-done((bf16[256,2048]{1,0:T(8,128)(2,1)S(1)}, bf16[256,2048]{1,0:T(8,128)(2,1)}, u32[]{:S(2)}) %copy-start.2) | copy-done | bytes 1048600
  76.4 0.0 copy-start.3
  76.4 1.2 %copy-done.3 = bf16[256,2048]{1,0:T(8,128)(2,1)S(1)} copy-done((bf16[256,2048]{1,0:T(8,128)(2,1)S(1)}, bf16[256,2048]{1,0:T(8,128)(2,1)}, u32[]{:S(2)}) %copy-start.3) | copy-done | bytes 1048600
  77.7 8.9 %finish.1 = (bf16[1,2048,768]{2,1,0:T(8,128)(2,1)}, bf16[1,2048,768]{2,1,0:T(8,128)(2,1)}, bf16[1,768,2048]{2,1,0:T(8,128)(2,1)}, bf16[256,2048]{1,0:T(8,128)(2,1)}, bf16[256,2048]{1,0:T(8,128)(2,1)}) custom-call(s32[1]{0:T(128)} %select_n.17.lead_ref, bf16[256,2048]{1,0:T(8,128)(2,1)S(1)} %copy-done, bf16[256,2048]{1,0:T(8,128)(2,1)S(1)} %copy-done.3, ...), custom_call_target="tpu_custom_call" | custom-call | tf_op jit(solution)/shard_map/finish/pallas_call | solution.py:317
  (4 shorter events, 0.0 us)
Async XLA Ops:
  2.0 71.7 %copy-start = (bf16[256,2048]{1,0:T(8,128)(2,1)S(1)}, bf16[256,2048]{1,0:T(8,128)(2,1)}, u32[]{:S(2)}) copy-start(bf16[256,2048]{1,0:T(8,128)(2,1)} %x.1) | copy-start | bytes 3145732
  73.6 1.6 %copy-start.1 = (bf16[512,2048]{1,0:T(8,128)(2,1)S(1)}, bf16[512,2048]{1,0:T(8,128)(2,1)}, u32[]{:S(2)}) copy-start(bf16[512,2048]{1,0:T(8,128)(2,1)} %get-tuple-element.26.og) | copy-start | bytes 6291460
  75.2 1.2 %copy-start.2 = (bf16[256,2048]{1,0:T(8,128)(2,1)S(1)}, bf16[256,2048]{1,0:T(8,128)(2,1)}, u32[]{:S(2)}) copy-start(bf16[256,2048]{1,0:T(8,128)(2,1)} %get-tuple-element.30.back_ing) | copy-start | bytes 3145732
  76.4 1.2 %copy-start.3 = (bf16[256,2048]{1,0:T(8,128)(2,1)S(1)}, bf16[256,2048]{1,0:T(8,128)(2,1)}, u32[]{:S(2)}) copy-start(bf16[256,2048]{1,0:T(8,128)(2,1)} %get-tuple-element.22.far_x) | copy-start | bytes 3145732

commit v3 on v2

v3 whole, which is shorter than its diff:
```python
import functools

import jax
import jax.numpy as jnp
from jax import lax
from jax.experimental import pallas as pl
from jax.experimental.pallas import tpu as pltpu
from jax.sharding import PartitionSpec as P

AXES = ("rows", "grp")
MESH = pl.DeviceIdType.MESH
F32 = jnp.float32
BF16 = jnp.bfloat16
X_CHUNKS = (32, 32, 64, 64, 64)
C_CHUNKS = (64, 64, 64, 32, 32)
HT = 256
DT = 512


def spans(sizes):
    start, out = 0, []
    for size in sizes:
        out.append((start, size))
        start += size
    return out


def dot(left, right):
    return jnp.dot(left, right, preferred_element_type=F32)


def dot_cols(left, right):
    return lax.dot_general(left, right, (((1,), (1,)), ((), ())), preferred_element_type=F32)


def dot_rows(left, right):
    return lax.dot_general(left, right, (((0,), (0,)), ((), ())), preferred_element_type=F32)


def tiles(extent, width):
    return [pl.ds(lo, width) for lo in range(0, extent, width)]


def to_column(row):
    return jnp.broadcast_to(row, (128, row.shape[1])).T


def exchange_kernel(
    sizes,
    starts, combine, x_hbm, cot_hbm, wg_hbm, wu_hbm, wd_hbm,
    mixed, ing, comb, grad_gate, grad_up, grad_down,
    wg, wu, wd, x, cot, scale_out, scale_in, own_col, far_col,
    gate, up, far_gate, far_up, far_out, hid, gg, ug, og,
    send_mixed, send_ing, back_mixed, back_ing, own_comb, far_comb, comb_out, comb_in,
    load_sem, scale_sem, x_sem, c_sem, m_sem, i_sem, comb_sem,
):
    n_rows, n_grp = sizes
    last = n_rows * n_grp - 1
    count, d = x_hbm.shape
    h = gate.shape[1]
    own, far = pl.ds(0, count), pl.ds(count, count)
    me = lax.axis_index("rows") * n_grp + lax.axis_index("grp")
    has_left, has_right = me > 0, me < last
    left = lax.rem(me + last, last + 1)
    right = lax.rem(me + 1, last + 1)
    left_id = (left // n_grp, lax.rem(left, n_grp))
    right_id = (right // n_grp, lax.rem(right, n_grp))

    loads = [
        pltpu.make_async_copy(src, dst, load_sem.at[i])
        for i, (src, dst) in enumerate(
            (
                (wg_hbm, wg),
                (wu_hbm, wu),
                (wd_hbm, wd),
                (x_hbm, x.at[own]),
                (cot_hbm, cot.at[own]),
            )
        )
    ]
    for load in loads:
        load.start()

    barrier = pltpu.get_barrier_semaphore()

    @pl.when(has_left)
    def _():
        pl.semaphore_signal(barrier, inc=1, device_id=left_id, device_id_type=MESH)

    @pl.when(has_right)
    def _():
        pl.semaphore_signal(barrier, inc=1, device_id=right_id, device_id_type=MESH)

    lead_count = lax.rem(starts[0], count)
    row_lead = lax.broadcasted_iota(jnp.int32, (1, count), 1) < lead_count
    scale = combine[...].astype(F32).reshape(1, count)
    zero_row = jnp.zeros_like(scale)
    scale_out[...] = jnp.broadcast_to(jnp.where(row_lead, scale, zero_row), scale_out.shape)
    own_col[...] = to_column(jnp.where(row_lead, zero_row, scale))

    @pl.when(has_left & has_right)
    def _():
        pl.semaphore_wait(barrier, 2)

    @pl.when(jnp.logical_not(has_left & has_right))
    def _():
        pl.semaphore_wait(barrier, 1)

    def remote(src, dst, sems, index, peer):
        return pltpu.make_async_remote_copy(
            src_ref=src,
            dst_ref=dst,
            send_sem=sems.at[0, index],
            recv_sem=sems.at[1, index],
            device_id=peer,
            device_id_type=MESH,
        )

    scale_copy = remote(scale_out, scale_in, scale_sem, 0, left_id)
    x_copies = [
        remote(x_hbm.at[pl.ds(lo, size)], x.at[pl.ds(count + lo, size)], x_sem, i, left_id)
        for i, (lo, size) in enumerate(spans(X_CHUNKS))
    ]
    c_copies = [
        remote(cot_hbm.at[pl.ds(lo, size)], cot.at[pl.ds(count + lo, size)], c_sem, i, left_id)
        for i, (lo, size) in enumerate(spans(C_CHUNKS))
    ]
    m_copies = [
        remote(send_mixed.at[pl.ds(lo, size)], back_mixed.at[pl.ds(lo, size)], m_sem, i, right_id)
        for i, (lo, size) in enumerate(spans(X_CHUNKS))
    ]
    i_copies = [
        remote(send_ing.at[pl.ds(lo, size)], back_ing.at[pl.ds(lo, size)], i_sem, i, right_id)
        for i, (lo, size) in enumerate(spans(C_CHUNKS))
    ]
    comb_copy = remote(comb_out, comb_in, comb_sem, 0, right_id)

    @pl.when(has_left)
    def _():
        scale_copy.start()
        for copy in x_copies + c_copies:
            copy.start()

    @pl.when(jnp.logical_not(has_right))
    def _():
        scale_in[...] = jnp.zeros_like(scale_in)
        x[far, :] = jnp.zeros((count, d), BF16)
        cot[far, :] = jnp.zeros((count, d), BF16)

    @pl.when(jnp.logical_not(has_left))
    def _():
        comb_in[...] = jnp.zeros_like(comb_in)
        back_mixed[...] = jnp.zeros_like(back_mixed)
        back_ing[...] = jnp.zeros_like(back_ing)

    def arrive(copy):
        pl.when(has_right)(copy.wait_recv)

    def send_back(copy):
        pl.when(has_right)(copy.start)

    loads[0].wait()
    loads[1].wait()

    def gate_up(at, gate_ref, up_ref, act_at):
        for cols in tiles(h, HT):
            rows = x[at, :]
            g = dot(rows, wg[:, cols])
            u = dot(rows, wu[:, cols])
            gate_ref[act_at, cols] = g
            up_ref[act_at, cols] = u
            hid[at, cols] = (g * jax.nn.sigmoid(g) * u).astype(BF16)

    def hidden_grads(at, act_at, gate_ref, up_ref):
        for cols in tiles(h, HT):
            hg = dot_cols(og[at, :], wd[cols, :])
            g, u = gate_ref[act_at, cols], up_ref[act_at, cols]
            s = jax.nn.sigmoid(g)
            gg[at, cols] = (hg * u * s * (1.0 + g * (1.0 - s))).astype(BF16)
            ug[at, cols] = (hg * (g * s)).astype(BF16)

    def input_grads(at, out_ref, out_at):
        for cols in tiles(d, DT):
            total = dot_cols(gg[at, :], wg[cols, :]) + dot_cols(ug[at, :], wu[cols, :])
            out_ref[out_at, cols] = total.astype(BF16)

    def far_forward(lo, size):
        at, act_at = pl.ds(count + lo, size), pl.ds(lo, size)
        gate_up(at, far_gate, far_up, act_at)
        for cols in tiles(d, DT):
            out = dot(hid[at, :], wd[:, cols])
            far_out[act_at, cols] = out
            send_mixed[act_at, cols] = (far_col[act_at, 0:1] * out).astype(BF16)

    def far_backward(lo, size):
        at, act_at = pl.ds(count + lo, size), pl.ds(lo, size)
        total = jnp.zeros((size, 1), F32)
        for cols in tiles(d, DT):
            c = cot[at, cols].astype(F32)
            og[at, cols] = (far_col[act_at, 0:1] * c).astype(BF16)
            total = total + jnp.sum(far_out[act_at, cols] * c, axis=1, keepdims=True)
        far_comb[act_at, :] = jnp.broadcast_to(total, (size, 128))
        hidden_grads(at, act_at, far_gate, far_up)
        input_grads(at, send_ing, act_at)

    def own_forward():
        loads[3].wait()
        gate_up(own, gate, up, own)

    def own_down():
        loads[4].wait()
        total = jnp.zeros((count, 1), F32)
        for cols in tiles(d, DT):
            out = dot(hid[own, :], wd[:, cols])
            mixed[:, cols] = (own_col[:, 0:1] * out).astype(BF16)
            c = cot[own, cols].astype(F32)
            og[own, cols] = (own_col[:, 0:1] * c).astype(BF16)
            total = total + jnp.sum(out * c, axis=1, keepdims=True)
        own_comb[...] = jnp.broadcast_to(total, (count, 128))

    def own_hidden_grads():
        hidden_grads(own, own, gate, up)

    def own_input_grads():
        input_grads(own, ing, own)

    arrive(scale_copy)
    far_col[...] = to_column(scale_in[0:1, :])
    own_steps = [own_forward, own_down, own_hidden_grads, own_input_grads]
    for i, (lo, size) in enumerate(spans(X_CHUNKS)):
        arrive(x_copies[i])
        if i == 0:
            loads[2].wait()
        far_forward(lo, size)
        send_back(m_copies[i])
        if i > 0 and own_steps:
            own_steps.pop(0)()
    for i, (lo, size) in enumerate(spans(C_CHUNKS)):
        arrive(c_copies[i])
        far_backward(lo, size)
        send_back(i_copies[i])
        if own_steps:
            own_steps.pop(0)()
    comb_out[...] = far_comb[...].T[0 : comb_out.shape[0], :]
    send_back(comb_copy)

    for cols in tiles(d, DT):
        rows = x[:, cols]
        grad_gate[cols, :] = dot_rows(rows, gg[...]).astype(BF16)
        grad_up[cols, :] = dot_rows(rows, ug[...]).astype(BF16)
    for cols in tiles(d, DT):
        grad_down[:, cols] = dot_rows(hid[...], og[:, cols]).astype(BF16)

    def select(back, out, lo, size):
        at = pl.ds(lo, size)
        lead = lax.broadcasted_iota(jnp.int32, (size, d), 0) + lo < lead_count
        out[at, :] = jnp.where(lead, back[at, :], out[at, :])

    for copies, back, out, sizes_ in (
        (m_copies, back_mixed, mixed, X_CHUNKS),
        (i_copies, back_ing, ing, C_CHUNKS),
    ):
        for copy, (lo, size) in zip(copies, spans(sizes_)):
            pl.when(has_left)(copy.wait_recv)
            select(back, out, lo, size)
    pl.when(has_left)(comb_copy.wait_recv)
    comb[...] = jnp.where(
        jnp.broadcast_to(row_lead, comb.shape), comb_in[...], own_comb[...].T[0 : comb.shape[0], :]
    )

    @pl.when(has_left)
    def _():
        for copy in [scale_copy] + x_copies + c_copies:
            copy.wait_send()

    @pl.when(has_right)
    def _():
        for copy in m_copies + i_copies + [comb_copy]:
            copy.wait_send()


def exchange(sizes, starts, combine, x, cot, wg, wu, wd):
    count, d = x.shape
    h = wg.shape[1]
    anywhere = pl.BlockSpec(memory_space=pl.ANY)
    vmem = pl.BlockSpec(memory_space=pltpu.VMEM)
    smem = pl.BlockSpec(memory_space=pltpu.SMEM)
    dma = pltpu.SemaphoreType.DMA
    return pl.pallas_call(
        functools.partial(exchange_kernel, sizes),
        name="exchange",
        out_shape=(
            jax.ShapeDtypeStruct((count, d), BF16),
            jax.ShapeDtypeStruct((count, d), BF16),
            jax.ShapeDtypeStruct((8, count), F32),
            jax.ShapeDtypeStruct((d, h), BF16),
            jax.ShapeDtypeStruct((d, h), BF16),
            jax.ShapeDtypeStruct((h, d), BF16),
        ),
        in_specs=[smem, vmem] + [pl.BlockSpec(memory_space=pltpu.HBM)] * 5,
        out_specs=(vmem,) * 6,
        scratch_shapes=[
            pltpu.VMEM((d, h), BF16),
            pltpu.VMEM((d, h), BF16),
            pltpu.VMEM((h, d), BF16),
            pltpu.VMEM((2 * count, d), BF16),
            pltpu.VMEM((2 * count, d), BF16),
            pltpu.VMEM((8, count), F32),
            pltpu.VMEM((8, count), F32),
            pltpu.VMEM((count, 128), F32),
            pltpu.VMEM((count, 128), F32),
            pltpu.VMEM((count, h), F32),
            pltpu.VMEM((count, h), F32),
            pltpu.VMEM((count, h), F32),
            pltpu.VMEM((count, h), F32),
            pltpu.VMEM((count, d), F32),
            pltpu.VMEM((2 * count, h), BF16),
            pltpu.VMEM((2 * count, h), BF16),
            pltpu.VMEM((2 * count, h), BF16),
            pltpu.VMEM((2 * count, d), BF16),
            pltpu.VMEM((count, d), BF16),
            pltpu.VMEM((count, d), BF16),
            pltpu.VMEM((count, d), BF16),
            pltpu.VMEM((count, d), BF16),
            pltpu.VMEM((count, 128), F32),
            pltpu.VMEM((count, 128), F32),
            pltpu.VMEM((8, count), F32),
            pltpu.VMEM((8, count), F32),
            dma((5,)),
            dma((2, 1)),
            dma((2, len(X_CHUNKS))),
            dma((2, len(C_CHUNKS))),
            dma((2, len(X_CHUNKS))),
            dma((2, len(C_CHUNKS))),
            dma((2, 1)),
        ],
        compiler_params=pltpu.CompilerParams(
            collective_id=0, has_side_effects=True, vmem_limit_bytes=30 * 2**20
        ),
    )(starts, combine, *(pltpu.with_memory_space_constraint(a, pltpu.HBM) for a in (x, cot, wg, wu, wd)))


def finish_kernel(mixed, ing, comb, gate, up, down, mixed_o, ing_o, comb_o, gate_o, up_o, down_o, sem):
    copies = [
        pltpu.make_async_copy(src, dst, sem.at[i])
        for i, (src, dst) in enumerate(
            ((gate, gate_o.at[0]), (up, up_o.at[0]), (down, down_o.at[0]), (mixed, mixed_o), (ing, ing_o))
        )
    ]
    for copy in copies:
        copy.start()
    comb_o[...] = comb[0:1, :].reshape(comb_o.shape).astype(BF16)
    for copy in copies:
        copy.wait()


def finish(mixed, ing, comb, gate, up, down):
    anywhere = pl.BlockSpec(memory_space=pl.ANY)
    vmem = pl.BlockSpec(memory_space=pltpu.VMEM)
    return pl.pallas_call(
        finish_kernel,
        name="finish",
        out_shape=(
            jax.ShapeDtypeStruct(mixed.shape, BF16),
            jax.ShapeDtypeStruct(ing.shape, BF16),
            jax.ShapeDtypeStruct(comb.shape[1:], BF16),
            jax.ShapeDtypeStruct((1,) + gate.shape, BF16),
            jax.ShapeDtypeStruct((1,) + up.shape, BF16),
            jax.ShapeDtypeStruct((1,) + down.shape, BF16),
        ),
        in_specs=[vmem] * 6,
        out_specs=(anywhere, anywhere, vmem) + (anywhere,) * 3,
        scratch_shapes=[pltpu.SemaphoreType.DMA((5,))],
        compiler_params=pltpu.CompilerParams(vmem_limit_bytes=2 * 2**20),
    )(*(pltpu.with_memory_space_constraint(a, pltpu.VMEM) for a in (mixed, ing, comb, gate, up, down)))


def solution(mesh):
    sizes = tuple(mesh.shape[axis] for axis in AXES)

    def on_device(sorted_rows, combine, cotangent, starts, w_gate, w_up, w_down):
        mixed, ing, comb, gate, up, down = exchange(
            sizes, starts, combine, sorted_rows, cotangent, w_gate[0], w_up[0], w_down[0]
        )
        mixed, ing, comb, gate, up, down = finish(mixed, ing, comb, gate, up, down)
        return mixed, comb, ing, gate, up, down

    rows2, rows1, rows3 = P(AXES, None), P(AXES), P(AXES, None, None)
    return jax.shard_map(
        on_device,
        mesh=mesh,
        in_specs=(rows2, rows1, rows2, rows1, rows3, rows3, rows3),
        out_specs=(rows2, rows1, rows2, rows3, rows3, rows3),
        check_vma=False,
    )
```

time: 86.8 us -> 73.4 us (0.85)
  the two profiles are of different devices: /device:TPU:0 before, /device:TPU:96 now
where the time goes in v3:
time: 73.4 us; the launch traced here: 73.3 us
  Pallas kernels  71.2 us (97%)
  between operations  1.46 us (2%)
    pallas_call x1, Pallas kernels, exchange(): pl.pallas_call(functools.partial(exchange_kernel, sizes), name='exchange'...  66.3 us
    pallas_call x1, Pallas kernels, finish(): pl.pallas_call(finish_kernel, name='finish', out_shape=(jax.ShapeDtypeStr...  4.86 us

profile of v3, /device:TPU:96, one launch (start us, length us, event | category | flops | bytes accessed | tf_op | source)
XLA Modules:
  0.0 73.3 jit_solution(12165872191740615515)
XLA Ops:
  1.3 0.0 copy-start
  1.3 0.6 copy-done
  1.9 66.3 %exchange.1 = (bf16[256,2048]{1,0:T(8,128)(2,1)S(1)}, bf16[256,2048]{1,0:T(8,128)(2,1)S(1)}, f32[8,256]{1,0:T(8,128)S(1)}, bf16[2048,768]{1,0:T(8,128)(2,1)S(1)}...) custom-call(s32[1]{0:T(128)S(6)} %copy.13.starts, bf16[256]{0:T(256)(128)(2,1)S(1)} %copy-done, ...), custom_call_target="tpu_custom_call" | custom-call | tf_op jit(solution)/shard_map/exchange/pallas_call | solution.py:289
  68.3 4.9 %finish.1 = (bf16[256,2048]{1,0:T(8,128)(2,1)}, bf16[256,2048]{1,0:T(8,128)(2,1)}, bf16[256]{0:T(256)(128)(2,1)}, bf16[1,2048,768]{2,1,0:T(8,128)(2,1)}, bf16[1,...) custom-call(bf16[256,2048]{1,0:T(8,128)(2,1)S(1)} %get-tuple-element.18.mixed, ...), custom_call_target="tpu_custom_call" | custom-call | tf_op jit(solution)/shard_map/finish/pallas_call | solution.py:360
Async XLA Ops:
  1.3 0.7 copy-start

commit v4 on v3

--- a/solution.py
+++ b/solution.py
@@ -11,26 +11,13 @@
 MESH = pl.DeviceIdType.MESH
 F32 = jnp.float32
 BF16 = jnp.bfloat16
-X_CHUNKS = (32, 32, 64, 64, 64)
-C_CHUNKS = (64, 64, 64, 32, 32)
+CHUNK = 32
 HT = 256
 DT = 512
 
 
-def spans(sizes):
-    start, out = 0, []
-    for size in sizes:
-        out.append((start, size))
-        start += size
-    return out
-
-
 def dot(left, right):
     return jnp.dot(left, right, preferred_element_type=F32)
-
-
-def dot_cols(left, right):
-    return lax.dot_general(left, right, (((1,), (1,)), ((), ())), preferred_element_type=F32)
 
 
 def dot_rows(left, right):
@@ -49,7 +36,7 @@
     sizes,
     starts, combine, x_hbm, cot_hbm, wg_hbm, wu_hbm, wd_hbm,
     mixed, ing, comb, grad_gate, grad_up, grad_down,
-    wg, wu, wd, x, cot, scale_out, scale_in, own_col, far_col,
+    wg, wu, wd, wg_t, wu_t, wd_t, x, cot, scale_out, scale_in, own_col, far_col,
     gate, up, far_gate, far_up, far_out, hid, gg, ug, og,
     send_mixed, send_ing, back_mixed, back_ing, own_comb, far_comb, comb_out, comb_in,
     load_sem, scale_sem, x_sem, c_sem, m_sem, i_sem, comb_sem,
@@ -117,29 +104,32 @@
         )
 
     scale_copy = remote(scale_out, scale_in, scale_sem, 0, left_id)
-    x_copies = [
-        remote(x_hbm.at[pl.ds(lo, size)], x.at[pl.ds(count + lo, size)], x_sem, i, left_id)
-        for i, (lo, size) in enumerate(spans(X_CHUNKS))
-    ]
-    c_copies = [
-        remote(cot_hbm.at[pl.ds(lo, size)], cot.at[pl.ds(count + lo, size)], c_sem, i, left_id)
-        for i, (lo, size) in enumerate(spans(C_CHUNKS))
-    ]
-    m_copies = [
-        remote(send_mixed.at[pl.ds(lo, size)], back_mixed.at[pl.ds(lo, size)], m_sem, i, right_id)
-        for i, (lo, size) in enumerate(spans(X_CHUNKS))
-    ]
-    i_copies = [
-        remote(send_ing.at[pl.ds(lo, size)], back_ing.at[pl.ds(lo, size)], i_sem, i, right_id)
-        for i, (lo, size) in enumerate(spans(C_CHUNKS))
-    ]
+    pieces = count // CHUNK
+
+    def piece(i, base=0):
+        return pl.ds(pl.multiple_of(base + i * CHUNK, CHUNK), CHUNK)
+
+    def x_copy(i):
+        return remote(x_hbm.at[piece(i)], x.at[piece(i, count)], x_sem, i, left_id)
+
+    def c_copy(i):
+        return remote(cot_hbm.at[piece(i)], cot.at[piece(i, count)], c_sem, i, left_id)
+
+    def m_copy(i):
+        return remote(send_mixed.at[piece(i)], back_mixed.at[piece(i)], m_sem, i, right_id)
+
+    def i_copy(i):
+        return remote(send_ing.at[piece(i)], back_ing.at[piece(i)], i_sem, i, right_id)
+
     comb_copy = remote(comb_out, comb_in, comb_sem, 0, right_id)
 
     @pl.when(has_left)
     def _():
         scale_copy.start()
-        for copy in x_copies + c_copies:
-            copy.start()
+        for i in range(pieces):
+            x_copy(i).start()
+        for i in range(pieces):
+            c_copy(i).start()
 
     @pl.when(jnp.logical_not(has_right))
     def _():
@@ -158,9 +148,6 @@
 
     def send_back(copy):
         pl.when(has_right)(copy.start)
-
-    loads[0].wait()
-    loads[1].wait()
 
     def gate_up(at, gate_ref, up_ref, act_at):
         for cols in tiles(h, HT):
@@ -173,7 +160,7 @@
 
     def hidden_grads(at, act_at, gate_ref, up_ref):
         for cols in tiles(h, HT):
-            hg = dot_cols(og[at, :], wd[cols, :])
+            hg = dot(og[at, :], wd_t[:, cols])
             g, u = gate_ref[act_at, cols], up_ref[act_at, cols]
             s = jax.nn.sigmoid(g)
             gg[at, cols] = (hg * u * s * (1.0 + g * (1.0 - s))).astype(BF16)
@@ -181,34 +168,32 @@
 
     def input_grads(at, out_ref, out_at):
         for cols in tiles(d, DT):
-            total = dot_cols(gg[at, :], wg[cols, :]) + dot_cols(ug[at, :], wu[cols, :])
+            total = dot(gg[at, :], wg_t[:, cols]) + dot(ug[at, :], wu_t[:, cols])
             out_ref[out_at, cols] = total.astype(BF16)
 
-    def far_forward(lo, size):
-        at, act_at = pl.ds(count + lo, size), pl.ds(lo, size)
+    def far_forward(i):
+        at, act_at = piece(i, count), piece(i)
         gate_up(at, far_gate, far_up, act_at)
         for cols in tiles(d, DT):
             out = dot(hid[at, :], wd[:, cols])
             far_out[act_at, cols] = out
             send_mixed[act_at, cols] = (far_col[act_at, 0:1] * out).astype(BF16)
 
-    def far_backward(lo, size):
-        at, act_at = pl.ds(count + lo, size), pl.ds(lo, size)
-        total = jnp.zeros((size, 1), F32)
+    def far_backward(i):
+        at, act_at = piece(i, count), piece(i)
+        total = jnp.zeros((CHUNK, 1), F32)
         for cols in tiles(d, DT):
             c = cot[at, cols].astype(F32)
             og[at, cols] = (far_col[act_at, 0:1] * c).astype(BF16)
             total = total + jnp.sum(far_out[act_at, cols] * c, axis=1, keepdims=True)
-        far_comb[act_at, :] = jnp.broadcast_to(total, (size, 128))
+        far_comb[act_at, :] = jnp.broadcast_to(total, (CHUNK, 128))
         hidden_grads(at, act_at, far_gate, far_up)
         input_grads(at, send_ing, act_at)
 
     def own_forward():
-        loads[3].wait()
         gate_up(own, gate, up, own)
 
     def own_down():
-        loads[4].wait()
         total = jnp.zeros((count, 1), F32)
         for cols in tiles(d, DT):
             out = dot(hid[own, :], wd[:, cols])
@@ -224,23 +209,37 @@
     def own_input_grads():
         input_grads(own, ing, own)
 
+    def transpose_down():
+        for cols in tiles(d, DT):
+            wd_t[cols, :] = wd[:, cols].T
+
+    loads[0].wait()
+    for cols in tiles(d, DT):
+        wg_t[:, cols] = wg[cols, :].T
+    loads[1].wait()
+    for cols in tiles(d, DT):
+        wu_t[:, cols] = wu[cols, :].T
+    for load in loads[2:]:
+        load.wait()
     arrive(scale_copy)
     far_col[...] = to_column(scale_in[0:1, :])
-    own_steps = [own_forward, own_down, own_hidden_grads, own_input_grads]
-    for i, (lo, size) in enumerate(spans(X_CHUNKS)):
-        arrive(x_copies[i])
-        if i == 0:
-            loads[2].wait()
-        far_forward(lo, size)
-        send_back(m_copies[i])
-        if i > 0 and own_steps:
-            own_steps.pop(0)()
-    for i, (lo, size) in enumerate(spans(C_CHUNKS)):
-        arrive(c_copies[i])
-        far_backward(lo, size)
-        send_back(i_copies[i])
-        if own_steps:
-            own_steps.pop(0)()
+
+    @pl.loop(0, pieces)
+    def _(i):
+        arrive(x_copy(i))
+        far_forward(i)
+        send_back(m_copy(i))
+        for k, step in enumerate((own_forward, own_down, transpose_down)):
+            pl.when(i == 2 * k + 1)(step)
+
+    @pl.loop(0, pieces)
+    def _(i):
+        arrive(c_copy(i))
+        far_backward(i)
+        send_back(i_copy(i))
+        for k, step in enumerate((own_hidden_grads, own_input_grads)):
+            pl.when(i == 2 * k + 1)(step)
+
     comb_out[...] = far_comb[...].T[0 : comb_out.shape[0], :]
     send_back(comb_copy)
 
@@ -251,18 +250,19 @@
     for cols in tiles(d, DT):
         grad_down[:, cols] = dot_rows(hid[...], og[:, cols]).astype(BF16)
 
-    def select(back, out, lo, size):
-        at = pl.ds(lo, size)
-        lead = lax.broadcasted_iota(jnp.int32, (size, d), 0) + lo < lead_count
-        out[at, :] = jnp.where(lead, back[at, :], out[at, :])
-
-    for copies, back, out, sizes_ in (
-        (m_copies, back_mixed, mixed, X_CHUNKS),
-        (i_copies, back_ing, ing, C_CHUNKS),
-    ):
-        for copy, (lo, size) in zip(copies, spans(sizes_)):
-            pl.when(has_left)(copy.wait_recv)
-            select(back, out, lo, size)
+    def select(copy, back, out, i):
+        pl.when(has_left)(copy(i).wait_recv)
+        lead = lax.broadcasted_iota(jnp.int32, (CHUNK, d), 0) + i * CHUNK < lead_count
+        out[piece(i), :] = jnp.where(lead, back[piece(i), :], out[piece(i), :])
+
+    @pl.loop(0, pieces)
+    def _(i):
+        select(m_copy, back_mixed, mixed, i)
+
+    @pl.loop(0, pieces)
+    def _(i):
+        select(i_copy, back_ing, ing, i)
+
     pl.when(has_left)(comb_copy.wait_recv)
     comb[...] = jnp.where(
         jnp.broadcast_to(row_lead, comb.shape), comb_in[...], own_comb[...].T[0 : comb.shape[0], :]
@@ -270,18 +270,23 @@
 
     @pl.when(has_left)
     def _():
-        for copy in [scale_copy] + x_copies + c_copies:
-            copy.wait_send()
+        scale_copy.wait_send()
+        for i in range(pieces):
+            x_copy(i).wait_send()
+            c_copy(i).wait_send()
 
     @pl.when(has_right)
     def _():
-        for copy in m_copies + i_copies + [comb_copy]:
-            copy.wait_send()
+        for i in range(pieces):
+            m_copy(i).wait_send()
+            i_copy(i).wait_send()
+        comb_copy.wait_send()
 
 
 def exchange(sizes, starts, combine, x, cot, wg, wu, wd):
     count, d = x.shape
     h = wg.shape[1]
+    pieces = count // CHUNK
     anywhere = pl.BlockSpec(memory_space=pl.ANY)
     vmem = pl.BlockSpec(memory_space=pltpu.VMEM)
     smem = pl.BlockSpec(memory_space=pltpu.SMEM)
@@ -303,6 +308,9 @@
             pltpu.VMEM((d, h), BF16),
             pltpu.VMEM((d, h), BF16),
             pltpu.VMEM((h, d), BF16),
+            pltpu.VMEM((h, d), BF16),
+            pltpu.VMEM((h, d), BF16),
+            pltpu.VMEM((d, h), BF16),
             pltpu.VMEM((2 * count, d), BF16),
             pltpu.VMEM((2 * count, d), BF16),
             pltpu.VMEM((8, count), F32),
@@ -328,14 +336,14 @@
             pltpu.VMEM((8, count), F32),
             dma((5,)),
             dma((2, 1)),
-            dma((2, len(X_CHUNKS))),
-            dma((2, len(C_CHUNKS))),
-            dma((2, len(X_CHUNKS))),
-            dma((2, len(C_CHUNKS))),
+            dma((2, pieces)),
+            dma((2, pieces)),
+            dma((2, pieces)),
+            dma((2, pieces)),
             dma((2, 1)),
         ],
         compiler_params=pltpu.CompilerParams(
-            collective_id=0, has_side_effects=True, vmem_limit_bytes=30 * 2**20
+            collective_id=0, has_side_effects=True, vmem_limit_bytes=40 * 2**20
         ),
     )(starts, combine, *(pltpu.with_memory_space_constraint(a, pltpu.HBM) for a in (x, cot, wg, wu, wd)))
 

time: 73.4 us -> 70.1 us (0.955)
  Pallas kernels: 71.2 us -> 68 us
    pallas_call x1, Pallas kernels: 66.3 us -> 63.1 us  [exchange(): pl.pallas_call(functools.partial(exchange_kernel, sizes), name='exchange'...]
where the time goes in v4:
time: 70.1 us; the launch traced here: 69.9 us
  Pallas kernels  68 us (97%)
  between operations  1.3 us (2%)
    pallas_call x1, Pallas kernels, exchange(): pl.pallas_call(functools.partial(exchange_kernel, sizes), name='exchange'...  63.1 us
    pallas_call x1, Pallas kernels, finish(): pl.pallas_call(finish_kernel, name='finish', out_shape=(jax.ShapeDtypeStr...  4.86 us

profile of v4, /device:TPU:96, one launch (start us, length us, event | category | flops | bytes accessed | tf_op | source)
XLA Modules:
  0.0 69.9 jit_solution(13205891348011899002)
XLA Ops:
  1.3 0.0 copy-start
  1.3 0.6 copy-done
  1.9 63.1 %exchange.1 = (bf16[256,2048]{1,0:T(8,128)(2,1)S(1)}, bf16[256,2048]{1,0:T(8,128)(2,1)S(1)}, f32[8,256]{1,0:T(8,128)S(1)}, bf16[2048,768]{1,0:T(8,128)(2,1)S(1)}...) custom-call(s32[1]{0:T(128)S(6)} %copy.13.starts, bf16[256]{0:T(256)(128)(2,1)S(1)} %copy-done, ...), custom_call_target="tpu_custom_call" | custom-call | tf_op jit(solution)/shard_map/exchange/pallas_call | solution.py:294
  65.1 4.9 %finish.1 = (bf16[256,2048]{1,0:T(8,128)(2,1)}, bf16[256,2048]{1,0:T(8,128)(2,1)}, bf16[256]{0:T(256)(128)(2,1)}, bf16[1,2048,768]{2,1,0:T(8,128)(2,1)}, bf16[1,...) custom-call(bf16[256,2048]{1,0:T(8,128)(2,1)S(1)} %get-tuple-element.18.mixed, ...), custom_call_target="tpu_custom_call" | custom-call | tf_op jit(solution)/shard_map/finish/pallas_call | solution.py:368
Async XLA Ops:
  1.3 0.7 copy-start

commit v5 on v4

--- a/solution.py
+++ b/solution.py
@@ -39,7 +39,7 @@
     wg, wu, wd, wg_t, wu_t, wd_t, x, cot, scale_out, scale_in, own_col, far_col,
     gate, up, far_gate, far_up, far_out, hid, gg, ug, og,
     send_mixed, send_ing, back_mixed, back_ing, own_comb, far_comb, comb_out, comb_in,
-    load_sem, scale_sem, x_sem, c_sem, m_sem, i_sem, comb_sem,
+    starts_s, combine_v, load_sem, scale_sem, x_sem, c_sem, m_sem, i_sem, comb_sem,
 ):
     n_rows, n_grp = sizes
     last = n_rows * n_grp - 1
@@ -53,6 +53,12 @@
     left_id = (left // n_grp, lax.rem(left, n_grp))
     right_id = (right // n_grp, lax.rem(right, n_grp))
 
+    small = [
+        pltpu.make_async_copy(starts, starts_s, load_sem.at[5]),
+        pltpu.make_async_copy(combine, combine_v, load_sem.at[6]),
+    ]
+    for load in small:
+        load.start()
     loads = [
         pltpu.make_async_copy(src, dst, load_sem.at[i])
         for i, (src, dst) in enumerate(
@@ -78,9 +84,11 @@
     def _():
         pl.semaphore_signal(barrier, inc=1, device_id=right_id, device_id_type=MESH)
 
-    lead_count = lax.rem(starts[0], count)
+    for load in small:
+        load.wait()
+    lead_count = lax.rem(starts_s[0], count)
     row_lead = lax.broadcasted_iota(jnp.int32, (1, count), 1) < lead_count
-    scale = combine[...].astype(F32).reshape(1, count)
+    scale = combine_v[...].astype(F32).reshape(1, count)
     zero_row = jnp.zeros_like(scale)
     scale_out[...] = jnp.broadcast_to(jnp.where(row_lead, scale, zero_row), scale_out.shape)
     own_col[...] = to_column(jnp.where(row_lead, zero_row, scale))
@@ -115,11 +123,15 @@
     def c_copy(i):
         return remote(cot_hbm.at[piece(i)], cot.at[piece(i, count)], c_sem, i, left_id)
 
-    def m_copy(i):
-        return remote(send_mixed.at[piece(i)], back_mixed.at[piece(i)], m_sem, i, right_id)
-
-    def i_copy(i):
-        return remote(send_ing.at[piece(i)], back_ing.at[piece(i)], i_sem, i, right_id)
+    def half_copy(src, dst, sems, i, half):
+        at = (piece(i), pl.ds(half * (d // 2), d // 2))
+        return remote(src.at[at], dst.at[at], sems, 2 * i + half, right_id)
+
+    def m_copy(i, half):
+        return half_copy(send_mixed, back_mixed, m_sem, i, half)
+
+    def i_copy(i, half):
+        return half_copy(send_ing, back_ing, i_sem, i, half)
 
     comb_copy = remote(comb_out, comb_in, comb_sem, 0, right_id)
 
@@ -149,8 +161,8 @@
     def send_back(copy):
         pl.when(has_right)(copy.start)
 
-    def gate_up(at, gate_ref, up_ref, act_at):
-        for cols in tiles(h, HT):
+    def gate_up(at, gate_ref, up_ref, act_at, spans):
+        for cols in spans:
             rows = x[at, :]
             g = dot(rows, wg[:, cols])
             u = dot(rows, wu[:, cols])
@@ -166,32 +178,36 @@
             gg[at, cols] = (hg * u * s * (1.0 + g * (1.0 - s))).astype(BF16)
             ug[at, cols] = (hg * (g * s)).astype(BF16)
 
-    def input_grads(at, out_ref, out_at):
-        for cols in tiles(d, DT):
+    def input_grads(at, out_ref, out_at, spans):
+        for cols in spans:
             total = dot(gg[at, :], wg_t[:, cols]) + dot(ug[at, :], wu_t[:, cols])
             out_ref[out_at, cols] = total.astype(BF16)
 
+    h_tiles, d_tiles = tiles(h, HT), tiles(d, DT)
+    d_halves = d_tiles[: len(d_tiles) // 2], d_tiles[len(d_tiles) // 2 :]
+
     def far_forward(i):
         at, act_at = piece(i, count), piece(i)
-        gate_up(at, far_gate, far_up, act_at)
-        for cols in tiles(d, DT):
-            out = dot(hid[at, :], wd[:, cols])
-            far_out[act_at, cols] = out
-            send_mixed[act_at, cols] = (far_col[act_at, 0:1] * out).astype(BF16)
+        gate_up(at, far_gate, far_up, act_at, h_tiles)
+        for half, spans in enumerate(d_halves):
+            for cols in spans:
+                out = dot(hid[at, :], wd[:, cols])
+                far_out[act_at, cols] = out
+                send_mixed[act_at, cols] = (far_col[act_at, 0:1] * out).astype(BF16)
+            send_back(m_copy(i, half))
 
     def far_backward(i):
         at, act_at = piece(i, count), piece(i)
         total = jnp.zeros((CHUNK, 1), F32)
-        for cols in tiles(d, DT):
+        for cols in d_tiles:
             c = cot[at, cols].astype(F32)
             og[at, cols] = (far_col[act_at, 0:1] * c).astype(BF16)
             total = total + jnp.sum(far_out[act_at, cols] * c, axis=1, keepdims=True)
         far_comb[act_at, :] = jnp.broadcast_to(total, (CHUNK, 128))
         hidden_grads(at, act_at, far_gate, far_up)
-        input_grads(at, send_ing, act_at)
-
-    def own_forward():
-        gate_up(own, gate, up, own)
+        for half, spans in enumerate(d_halves):
+            input_grads(at, send_ing, act_at, spans)
+            send_back(i_copy(i, half))
 
     def own_down():
         total = jnp.zeros((count, 1), F32)
@@ -203,23 +219,28 @@
             total = total + jnp.sum(out * c, axis=1, keepdims=True)
         own_comb[...] = jnp.broadcast_to(total, (count, 128))
 
-    def own_hidden_grads():
-        hidden_grads(own, own, gate, up)
-
-    def own_input_grads():
-        input_grads(own, ing, own)
+    def transpose(src, dst):
+        for cols in d_tiles:
+            dst[:, cols] = src[cols, :].T
 
     def transpose_down():
-        for cols in tiles(d, DT):
+        for cols in d_tiles:
             wd_t[cols, :] = wd[:, cols].T
 
-    loads[0].wait()
-    for cols in tiles(d, DT):
-        wg_t[:, cols] = wg[cols, :].T
-    loads[1].wait()
-    for cols in tiles(d, DT):
-        wu_t[:, cols] = wu[cols, :].T
-    for load in loads[2:]:
+    def own_gate_up(cols):
+        gate_up(own, gate, up, own, [cols])
+
+    forward_steps = [functools.partial(own_gate_up, cols) for cols in h_tiles] + [
+        own_down,
+        functools.partial(transpose, wg, wg_t),
+        functools.partial(transpose, wu, wu_t),
+        transpose_down,
+    ]
+    backward_steps = [functools.partial(hidden_grads, own, own, gate, up)] + [
+        functools.partial(input_grads, own, ing, own, spans) for spans in d_halves
+    ]
+
+    for load in loads:
         load.wait()
     arrive(scale_copy)
     far_col[...] = to_column(scale_in[0:1, :])
@@ -228,17 +249,15 @@
     def _(i):
         arrive(x_copy(i))
         far_forward(i)
-        send_back(m_copy(i))
-        for k, step in enumerate((own_forward, own_down, transpose_down)):
-            pl.when(i == 2 * k + 1)(step)
+        for k, step in enumerate(forward_steps):
+            pl.when(i == k)(step)
 
     @pl.loop(0, pieces)
     def _(i):
         arrive(c_copy(i))
         far_backward(i)
-        send_back(i_copy(i))
-        for k, step in enumerate((own_hidden_grads, own_input_grads)):
-            pl.when(i == 2 * k + 1)(step)
+        for k, step in enumerate(backward_steps):
+            pl.when(i == k)(step)
 
     comb_out[...] = far_comb[...].T[0 : comb_out.shape[0], :]
     send_back(comb_copy)
@@ -251,7 +270,8 @@
         grad_down[:, cols] = dot_rows(hid[...], og[:, cols]).astype(BF16)
 
     def select(copy, back, out, i):
-        pl.when(has_left)(copy(i).wait_recv)
+        for half in range(2):
+            pl.when(has_left)(copy(i, half).wait_recv)
         lead = lax.broadcasted_iota(jnp.int32, (CHUNK, d), 0) + i * CHUNK < lead_count
         out[piece(i), :] = jnp.where(lead, back[piece(i), :], out[piece(i), :])
 
@@ -278,8 +298,9 @@
     @pl.when(has_right)
     def _():
         for i in range(pieces):
-            m_copy(i).wait_send()
-            i_copy(i).wait_send()
+            for half in range(2):
+                m_copy(i, half).wait_send()
+                i_copy(i, half).wait_send()
         comb_copy.wait_send()
 
 
@@ -287,9 +308,7 @@
     count, d = x.shape
     h = wg.shape[1]
     pieces = count // CHUNK
-    anywhere = pl.BlockSpec(memory_space=pl.ANY)
     vmem = pl.BlockSpec(memory_space=pltpu.VMEM)
-    smem = pl.BlockSpec(memory_space=pltpu.SMEM)
     dma = pltpu.SemaphoreType.DMA
     return pl.pallas_call(
         functools.partial(exchange_kernel, sizes),
@@ -302,7 +321,7 @@
             jax.ShapeDtypeStruct((d, h), BF16),
             jax.ShapeDtypeStruct((h, d), BF16),
         ),
-        in_specs=[smem, vmem] + [pl.BlockSpec(memory_space=pltpu.HBM)] * 5,
+        in_specs=[pl.BlockSpec(memory_space=pl.ANY)] + [pl.BlockSpec(memory_space=pltpu.HBM)] * 6,
         out_specs=(vmem,) * 6,
         scratch_shapes=[
             pltpu.VMEM((d, h), BF16),
@@ -334,18 +353,20 @@
             pltpu.VMEM((count, 128), F32),
             pltpu.VMEM((8, count), F32),
             pltpu.VMEM((8, count), F32),
-            dma((5,)),
+            pltpu.SMEM((1,), jnp.int32),
+            pltpu.VMEM((count,), BF16),
+            dma((7,)),
             dma((2, 1)),
             dma((2, pieces)),
             dma((2, pieces)),
-            dma((2, pieces)),
-            dma((2, pieces)),
+            dma((2, 2 * pieces)),
+            dma((2, 2 * pieces)),
             dma((2, 1)),
         ],
         compiler_params=pltpu.CompilerParams(
             collective_id=0, has_side_effects=True, vmem_limit_bytes=40 * 2**20
         ),
-    )(starts, combine, *(pltpu.with_memory_space_constraint(a, pltpu.HBM) for a in (x, cot, wg, wu, wd)))
+    )(starts, *(pltpu.with_memory_space_constraint(a, pltpu.HBM) for a in (combine, x, cot, wg, wu, wd)))
 
 
 def finish_kernel(mixed, ing, comb, gate, up, down, mixed_o, ing_o, comb_o, gate_o, up_o, down_o, sem):

time: 70.1 us -> 69.1 us (0.986)
  no operation moved by 1% of the time
where the time goes in v5:
time: 69.1 us; the launch traced here: 69 us
  Pallas kernels  67.5 us (98%)
  between operations  1.45 us (2%)
    pallas_call x1, Pallas kernels, exchange(): pl.pallas_call(functools.partial(exchange_kernel, sizes), name='exchange'...  62.7 us
    pallas_call x1, Pallas kernels, finish(): pl.pallas_call(finish_kernel, name='finish', out_shape=(jax.ShapeDtypeStr...  4.86 us

profile of v5, /device:TPU:96, one launch (start us, length us, event | category | flops | bytes accessed | tf_op | source)
XLA Modules:
  0.0 69.0 jit_solution(5548569145296005562)
XLA Ops:
  1.3 62.7 %exchange.1 = (bf16[256,2048]{1,0:T(8,128)(2,1)S(1)}, bf16[256,2048]{1,0:T(8,128)(2,1)S(1)}, f32[8,256]{1,0:T(8,128)S(1)}, bf16[2048,768]{1,0:T(8,128)(2,1)S(1)}...) custom-call(s32[1]{0:T(128)S(6)} %copy.13.starts, bf16[256]{0:T(256)(128)(2,1)} %combine.1, ...), custom_call_target="tpu_custom_call" | custom-call | tf_op jit(solution)/shard_map/exchange/pallas_call | solution.py:313
  64.0 4.9 %finish.1 = (bf16[256,2048]{1,0:T(8,128)(2,1)}, bf16[256,2048]{1,0:T(8,128)(2,1)}, bf16[256]{0:T(256)(128)(2,1)}, bf16[1,2048,768]{2,1,0:T(8,128)(2,1)}, bf16[1,...) custom-call(bf16[256,2048]{1,0:T(8,128)(2,1)S(1)} %get-tuple-element.18.mixed, ...), custom_call_target="tpu_custom_call" | custom-call | tf_op jit(solution)/shard_map/finish/pallas_call | solution.py:389

commit v6 on v5

--- a/solution.py
+++ b/solution.py
@@ -53,6 +53,16 @@
     left_id = (left // n_grp, lax.rem(left, n_grp))
     right_id = (right // n_grp, lax.rem(right, n_grp))
 
+    barrier = pltpu.get_barrier_semaphore()
+
+    @pl.when(has_left)
+    def _():
+        pl.semaphore_signal(barrier, inc=1, device_id=left_id, device_id_type=MESH)
+
+    @pl.when(has_right)
+    def _():
+        pl.semaphore_signal(barrier, inc=1, device_id=right_id, device_id_type=MESH)
+
     small = [
         pltpu.make_async_copy(starts, starts_s, load_sem.at[5]),
         pltpu.make_async_copy(combine, combine_v, load_sem.at[6]),
@@ -74,16 +84,6 @@
     for load in loads:
         load.start()
 
-    barrier = pltpu.get_barrier_semaphore()
-
-    @pl.when(has_left)
-    def _():
-        pl.semaphore_signal(barrier, inc=1, device_id=left_id, device_id_type=MESH)
-
-    @pl.when(has_right)
-    def _():
-        pl.semaphore_signal(barrier, inc=1, device_id=right_id, device_id_type=MESH)
-
     for load in small:
         load.wait()
     lead_count = lax.rem(starts_s[0], count)
@@ -279,15 +279,6 @@
     def _(i):
         select(m_copy, back_mixed, mixed, i)
 
-    @pl.loop(0, pieces)
-    def _(i):
-        select(i_copy, back_ing, ing, i)
-
-    pl.when(has_left)(comb_copy.wait_recv)
-    comb[...] = jnp.where(
-        jnp.broadcast_to(row_lead, comb.shape), comb_in[...], own_comb[...].T[0 : comb.shape[0], :]
-    )
-
     @pl.when(has_left)
     def _():
         scale_copy.wait_send()
@@ -302,6 +293,17 @@
                 m_copy(i, half).wait_send()
                 i_copy(i, half).wait_send()
         comb_copy.wait_send()
+
+    comb[...] = own_comb[...].T[0 : comb.shape[0], :]
+
+    @pl.loop(0, pieces)
+    def _(i):
+        select(i_copy, back_ing, ing, i)
+
+    pl.when(has_left)(comb_copy.wait_recv)
+    comb[...] = jnp.where(
+        jnp.broadcast_to(row_lead, comb.shape), comb_in[...], comb[...]
+    )
 
 
 def exchange(sizes, starts, combine, x, cot, wg, wu, wd):

time: 69.1 us -> 68.9 us (level)
  no operation moved by 1% of the time
where the time goes in v6:
time: 68.9 us; the launch traced here: 68.8 us
  Pallas kernels  67.4 us (98%)
  between operations  1.45 us (2%)
    pallas_call x1, Pallas kernels, exchange(): pl.pallas_call(functools.partial(exchange_kernel, sizes), name='exchange'...  62.5 us
    pallas_call x1, Pallas kernels, finish(): pl.pallas_call(finish_kernel, name='finish', out_shape=(jax.ShapeDtypeStr...  4.86 us

profile of v6, /device:TPU:96, one launch (start us, length us, event | category | flops | bytes accessed | tf_op | source)
XLA Modules:
  0.0 68.8 jit_solution(11377401133776456996)
XLA Ops:
  1.3 62.5 %exchange.1 = (bf16[256,2048]{1,0:T(8,128)(2,1)S(1)}, bf16[256,2048]{1,0:T(8,128)(2,1)S(1)}, f32[8,256]{1,0:T(8,128)S(1)}, bf16[2048,768]{1,0:T(8,128)(2,1)S(1)}...) custom-call(s32[1]{0:T(128)S(6)} %copy.13.starts, bf16[256]{0:T(256)(128)(2,1)} %combine.1, ...), custom_call_target="tpu_custom_call" | custom-call | tf_op jit(solution)/shard_map/exchange/pallas_call | solution.py:315
  63.8 4.9 %finish.1 = (bf16[256,2048]{1,0:T(8,128)(2,1)}, bf16[256,2048]{1,0:T(8,128)(2,1)}, bf16[256]{0:T(256)(128)(2,1)}, bf16[1,2048,768]{2,1,0:T(8,128)(2,1)}, bf16[1,...) custom-call(bf16[256,2048]{1,0:T(8,128)(2,1)S(1)} %get-tuple-element.18.mixed, ...), custom_call_target="tpu_custom_call" | custom-call | tf_op jit(solution)/shard_map/finish/pallas_call | solution.py:391

commit v7 on v6

--- a/solution.py
+++ b/solution.py
@@ -64,7 +64,6 @@
         pl.semaphore_signal(barrier, inc=1, device_id=right_id, device_id_type=MESH)
 
     small = [
-        pltpu.make_async_copy(starts, starts_s, load_sem.at[5]),
         pltpu.make_async_copy(combine, combine_v, load_sem.at[6]),
     ]
     for load in small:
@@ -86,7 +85,7 @@
 
     for load in small:
         load.wait()
-    lead_count = lax.rem(starts_s[0], count)
+    lead_count = lax.rem(starts[0:1, 0:1], count)
     row_lead = lax.broadcasted_iota(jnp.int32, (1, count), 1) < lead_count
     scale = combine_v[...].astype(F32).reshape(1, count)
     zero_row = jnp.zeros_like(scale)
@@ -323,7 +322,7 @@
             jax.ShapeDtypeStruct((d, h), BF16),
             jax.ShapeDtypeStruct((h, d), BF16),
         ),
-        in_specs=[pl.BlockSpec(memory_space=pl.ANY)] + [pl.BlockSpec(memory_space=pltpu.HBM)] * 6,
+        in_specs=[vmem] + [pl.BlockSpec(memory_space=pltpu.HBM)] * 6,
         out_specs=(vmem,) * 6,
         scratch_shapes=[
             pltpu.VMEM((d, h), BF16),
@@ -368,7 +367,7 @@
         compiler_params=pltpu.CompilerParams(
             collective_id=0, has_side_effects=True, vmem_limit_bytes=40 * 2**20
         ),
-    )(starts, *(pltpu.with_memory_space_constraint(a, pltpu.HBM) for a in (combine, x, cot, wg, wu, wd)))
+    )(jnp.broadcast_to(starts, (8, 128)), *(pltpu.with_memory_space_constraint(a, pltpu.HBM) for a in (combine, x, cot, wg, wu, wd)))
 
 
 def finish_kernel(mixed, ing, comb, gate, up, down, mixed_o, ing_o, comb_o, gate_o, up_o, down_o, sem):

time: 68.9 us -> 68.9 us (level)
  no operation moved by 1% of the time
where the time goes in v7:
time: 68.9 us; the launch traced here: 68.8 us
  Pallas kernels  67.4 us (98%)
  between operations  1.45 us (2%)
    pallas_call x1, Pallas kernels, exchange(): pl.pallas_call(functools.partial(exchange_kernel, sizes), name='exchange'...  62.5 us
    pallas_call x1, Pallas kernels, finish(): pl.pallas_call(finish_kernel, name='finish', out_shape=(jax.ShapeDtypeStr...  4.86 us

profile of v7, /device:TPU:96, one launch (start us, length us, event | category | flops | bytes accessed | tf_op | source)
XLA Modules:
  0.0 68.8 jit_solution(4263415483523538703)
XLA Ops:
  1.3 62.5 %exchange.1 = (bf16[256,2048]{1,0:T(8,128)(2,1)S(1)}, bf16[256,2048]{1,0:T(8,128)(2,1)S(1)}, f32[8,256]{1,0:T(8,128)S(1)}, bf16[2048,768]{1,0:T(8,128)(2,1)S(1)}...) custom-call(s32[8,128]{1,0:T(8,128)S(1)} %broadcast_in_dim.2.starts, bf16[256]{0:T(256)(128)(2,1)} %combine.1, ...), custom_call_target="tpu_custom_call" | custom-call | tf_op jit(solution)/shard_map/exchange/pallas_call | solution.py:314
  63.8 4.9 %finish.1 = (bf16[256,2048]{1,0:T(8,128)(2,1)}, bf16[256,2048]{1,0:T(8,128)(2,1)}, bf16[256]{0:T(256)(128)(2,1)}, bf16[1,2048,768]{2,1,0:T(8,128)(2,1)}, bf16[1,...) custom-call(bf16[256,2048]{1,0:T(8,128)(2,1)S(1)} %get-tuple-element.18.mixed, ...), custom_call_target="tpu_custom_call" | custom-call | tf_op jit(solution)/shard_map/finish/pallas_call | solution.py:390
  (1 shorter events, 0.0 us)
